TPU v7x, 512 devices: a whole 4x8x8 slice. The times are simulated.
512 devices in a mesh: req: 128 (over z, y, core), mlp: 4 (over x).
Axes of the slice: x: 4, y: 8, z: 8, core: 2. Of those that a mesh axis runs over, the one named last changes fastest.
Arguments:
- patches: bfloat16 [16384, 4, 1280], P('req', 'mlp'), may hold values from -6 to 6
- vis_gain: float32 [1280], replicated, may hold values from 0.5 to 1.5
- proj_weight: bfloat16 [4, 1280, 1280], P('mlp', 'req'), may hold values from -0.078125 to 0.078125
- image_dest: int32 [16384, 1], P('req'), may hold values from 0 to 127; in each aligned block of 128 rows (0 to 127, 128 to 255, ...) at most 2 rows name the same one
- image_pos: int32 [128], P('req'), may hold values from 0 to 255
- text_len: int32 [128], P('req'), may hold values from 64 to 255
- text: bfloat16 [128, 256, 1280], P('req'), may hold values from -6 to 6
- attn_gain: float32 [1280], replicated, may hold values from 0.5 to 1.5
- qkv_weight: bfloat16 [3, 1280, 1280], P(None, 'req', 'mlp'), may hold values from -0.15625 to 0.15625
- out_weight: bfloat16 [1280, 1280], P('mlp', 'req'), may hold values from -0.15625 to 0.15625
- cache_keys: bfloat16 [128, 1280, 1280], P('req', None, 'mlp')
- cache_values: bfloat16 [128, 1280, 1280], P('req', None, 'mlp'), may hold values from -6 to 6
- held: bfloat16 [16384, 1280], P('req'), may hold values from -6 to 6
- held_owner: int32 [128, 128, 1], P('req'), may hold values from 0 to 127; in each aligned block of 128 rows (0 to 127, 128 to 255, ..., all dimensions but the last counted through in order) at most 2 rows name the same one
- held_row: int32 [128, 128], P('req'), may hold values from 0 to 127
- recompute_pos: int32 [128, 128], P('req'), may hold values from 0 to 1279, as said below
Outputs:
- attended: bfloat16 [128, 256, 1280], P('req', None, 'mlp')
Inputs may be any that keep to these rules, and one draw needn't show every extreme that they name: `image_dest`: within each aligned block of 128 rows no request is named more than 2 times. `held_owner`: within each request's 128 rows no owner is named more than 2 times. `recompute_pos`: the positions of one request are distinct.
All inputs are finite; a program needn't handle non-finite values.
Results may differ from a plain program's by a relative error of at most 0.013.
The roundings to bfloat16 on the way count: a program that leaves them out, or rounds other values in their place, can miss the bound.
Values may be sent and summed in bfloat16 or wider, within the bound.
A program may use at most 128 MiB of HBM per device.

v0:
```python
import jax
import jax.numpy as jnp
from jax import lax
from jax.sharding import PartitionSpec as P

HEAD_DIM = 80


eps = 1e-06
big_negative = -1e30


def norm_rows(values, gain):
    floats = values.astype(jnp.float32)
    return (floats * lax.rsqrt(jnp.mean(floats * floats, -1, keepdims=True) + eps) * gain).astype(
        jnp.bfloat16
    )


def attend(queries, all_keys, all_values, length):
    seq_len = queries.shape[0]
    cache_len = all_keys.shape[0] - seq_len
    head_count = queries.shape[1] // HEAD_DIM
    query_heads = queries.reshape(seq_len, head_count, HEAD_DIM)
    key_heads = all_keys.reshape(-1, head_count, HEAD_DIM)
    value_heads = all_values.reshape(-1, head_count, HEAD_DIM)
    scores = jnp.einsum(
        "qhd,khd->hqk", query_heads, key_heads, preferred_element_type=jnp.float32
    ) * HEAD_DIM ** (-0.5)
    row_ids = jnp.arange(seq_len, dtype=jnp.int32)[:, None]
    col_ids = jnp.arange(all_keys.shape[0], dtype=jnp.int32)[None, :] - cache_len
    allowed = (col_ids < 0) | (col_ids <= row_ids) & (col_ids < length)
    scores = jnp.where(allowed[None], scores, big_negative)
    highest = jnp.max(scores, -1, keepdims=True)
    weights = jnp.exp(scores - highest)
    weights = (weights / jnp.sum(weights, -1, keepdims=True)).astype(jnp.bfloat16)
    mixed = jnp.einsum(
        "hqk,khd->qhd", weights, value_heads, preferred_element_type=jnp.float32
    ).astype(jnp.bfloat16)
    mixed = mixed.reshape(seq_len, -1)
    return jnp.where(row_ids < length, mixed, jnp.zeros_like(mixed))


def slot_ranks(targets, groups):
    onehot = (targets[:, None] == jnp.arange(groups, dtype=jnp.int32)[None, :]).astype(jnp.int32)
    before = jnp.cumsum(onehot, 0) - onehot
    return (jnp.sum(before * onehot, 1), jnp.sum(onehot, 0))


def local(
    patches,
    vis_gain,
    proj_weight,
    image_dest,
    image_pos,
    text_len,
    text,
    attn_gain,
    qkv_weight,
    out_weight,
    cache_keys,
    cache_values,
    held,
    held_owner,
    held_row,
    recompute_pos,
):
    n_req = lax.axis_size("req")
    normed_patch = norm_rows(patches[:, 0, :], vis_gain)
    partial_image = jnp.dot(
        normed_patch,
        lax.all_gather(proj_weight, "req", axis=1, tiled=True)[0],
        preferred_element_type=jnp.float32,
    )
    image_tokens = lax.psum_scatter(partial_image, "mlp", scatter_dimension=1, tiled=True).astype(
        jnp.bfloat16
    )
    img_dev = image_tokens.shape[0]
    capacity = max(2, 2 * img_dev // n_req)
    targets = image_dest[:, 0]
    image_rank, image_counts = slot_ranks(targets, n_req)
    outgoing = (
        jnp.zeros((n_req, capacity, image_tokens.shape[1]), jnp.bfloat16)
        .at[targets, image_rank]
        .set(image_tokens)
    )
    arrived, arrived_counts = (
        lax.all_to_all(outgoing, "req", split_axis=0, concat_axis=0, tiled=True),
        lax.all_to_all(
            image_counts.reshape(n_req, 1), "req", split_axis=0, concat_axis=0, tiled=True
        ),
    )
    filled = (
        (jnp.arange(capacity, dtype=jnp.int32)[None, :] < arrived_counts)
        .reshape(-1)
        .astype(jnp.int32)
    )
    image_order = jnp.cumsum(filled) - filled
    img_count = jnp.sum(filled)
    arrived_rows = arrived.reshape(n_req * capacity, arrived.shape[2])
    arrived_rows = lax.all_gather(arrived_rows, "mlp", axis=1, tiled=True)
    seq_len = text.shape[1]
    spots = jnp.arange(seq_len, dtype=jnp.int32)
    offset = jnp.minimum(image_pos[0], seq_len - img_count)
    in_image = (spots >= offset) & (spots < offset + img_count)
    chooser = ((image_order[None, :] == (spots - offset)[:, None]) & (filled[None, :] > 0)).astype(
        jnp.bfloat16
    )
    image_part = jnp.dot(chooser, arrived_rows, preferred_element_type=jnp.float32).astype(
        jnp.bfloat16
    )
    text_index = jnp.clip(jnp.where(spots < offset, spots, spots - img_count), 0, seq_len - 1)
    prompt = jnp.where(in_image[:, None], image_part, text[0][text_index])
    length = jnp.minimum(seq_len, text_len[0] + img_count)
    normed = norm_rows(prompt, attn_gain)
    weight_cols = lax.all_gather(qkv_weight, "req", axis=1, tiled=True)
    queries = jnp.dot(normed, weight_cols[0], preferred_element_type=jnp.float32).astype(
        jnp.bfloat16
    )
    new_keys = jnp.dot(normed, weight_cols[1], preferred_element_type=jnp.float32).astype(
        jnp.bfloat16
    )
    new_values = jnp.dot(normed, weight_cols[2], preferred_element_type=jnp.float32).astype(
        jnp.bfloat16
    )
    owners = held_owner[0, :, 0]
    fetch_rank, fetch_counts = slot_ranks(owners, n_req)
    recomp = owners.shape[0]
    fetch_cap = max(2, 2 * recomp // n_req)
    wanted_rows = jnp.zeros((n_req, fetch_cap), jnp.int32).at[owners, fetch_rank].set(held_row[0])
    picked = held[lax.all_to_all(wanted_rows, "req", split_axis=0, concat_axis=0, tiled=True)]
    fetched = lax.all_to_all(picked, "req", split_axis=0, concat_axis=0, tiled=True)
    gotten = fetched[owners, fetch_rank]
    held_norm = norm_rows(gotten, attn_gain)
    fresh_keys = jnp.dot(held_norm, weight_cols[1], preferred_element_type=jnp.float32).astype(
        jnp.bfloat16
    )
    fresh_values = jnp.dot(held_norm, weight_cols[2], preferred_element_type=jnp.float32).astype(
        jnp.bfloat16
    )
    keys_now = cache_keys[0].at[recompute_pos[0]].set(fresh_keys)
    values_now = cache_values[0].at[recompute_pos[0]].set(fresh_values)
    mixed = attend(
        queries,
        jnp.concatenate([keys_now, new_keys], 0),
        jnp.concatenate([values_now, new_values], 0),
        length,
    )
    terms = jnp.dot(
        mixed,
        lax.all_gather(out_weight, "req", axis=1, tiled=True),
        preferred_element_type=jnp.float32,
    )
    result = lax.psum_scatter(terms, "mlp", scatter_dimension=1, tiled=True).astype(jnp.bfloat16)
    return result[None]


def solution(mesh):
    in_specs = (
        P("req", "mlp", None),
        P(),
        P("mlp", "req", None),
        P("req", None),
        P("req"),
        P("req"),
        P("req", None, None),
        P(),
        P(None, "req", "mlp"),
        P("mlp", "req"),
        P("req", None, "mlp"),
        P("req", None, "mlp"),
        P("req", None),
        P("req", None, None),
        P("req", None),
        P("req", None),
    )
    out_specs = P("req", None, "mlp")
    return jax.shard_map(local, mesh=mesh, in_specs=in_specs, out_specs=out_specs, check_vma=False)
```

profile of v0, /device:TPU:1, one launch (start us, length us, event | category | flops | bytes accessed | tf_op | source)
XLA Modules:
  0.0 346.0 jit_solution(4919640971527965085)
XLA Ops:
  6.6 1.5 copy.49
  11.4 18.4 %all-to-all-start = ((s32[128,1,1]{2,1,0:T(1,128)}), s32[128,1,1]{2,1,0:T(1,128)S(1)}, u32[]{:S(2)}, u32[]{:S(2)}) async-start(s32[128,1,1]{2,1,0:T(1,128)} %copy.44), calls=%async_computation | async-start | bytes 131072 | tf_op jit(solution)/shard_map/all_to_all | solution.py:89
  31.6 1.1 fusion.24
  32.7 53.2 %all-gather = bf16[128,10,320]{2,1,0:T(8,128)(2,1)S(1)} all-gather(bf16[1,10,320]{2,1,0:T(8,128)(2,1)} %bitcast.98), channel_id=1, replica_groups=mesh['req'=128,'mlp'=4] {'req'}, dimensions={0}, use_global_device_ids=true | all-gather | bytes 825600 | tf_op jit(solution)/shard_map/all_gather | solution.py:151
  87.3 6.4 %scatter_fusion = s32[128,2]{0,1:T(2,128)S(1)} fusion(s32[128,2]{0,1:T(2,128)S(1)} %broadcast.276, s32[128]{0:T(128)S(1)} %get-tuple-element.7, s32[128]{0:T(128)S(1)} %bitcast.105), kind=kCustom, calls=%fused_computation.3 | custom fusion | bytes 2560 | tf_op jit(solution)/shard_map/scatter | solution.py:130
  94.4 1.3 copy.55
  96.4 2.3 copy.45
  98.7 1.4 reshape.394
  100.1 9.7 %all-to-all-start.1 = ((s32[128,1,2]{2,1,0:T(1,128)}), s32[128,1,2]{2,1,0:T(1,128)S(1)}, u32[]{:S(2)}, u32[]{:S(2)}) async-start(s32[128,1,2]{2,1,0:T(1,128)} %copy.46), calls=%async_computation.1 | async-start | bytes 131072 | tf_op jit(solution)/shard_map/all_to_all | solution.py:131
  109.8 2.4 reduce.2
  114.6 6.6 %all-to-all-done.1 = s32[128,1,2]{2,1,0:T(1,128)S(1)} async-done(((s32[128,1,2]{2,1,0:T(1,128)}), s32[128,1,2]{2,1,0:T(1,128)S(1)}, u32[]{:S(2)}, u32[]{:S(2)}) %all-to-all-start.1) | async-done | bytes 1056 | tf_op jit(solution)/shard_map/all_to_all | solution.py:131
  121.4 1.2 gather_fusion
  122.7 1.1 reshape.343
  123.7 7.1 %all-to-all-start.2 = ((bf16[128,2,1280]{2,1,0:T(2,128)(2,1)}), bf16[128,2,1280]{2,1,0:T(2,128)(2,1)S(1)}, u32[]{:S(2)}, u32[]{:S(2)}) async-start(bf16[128,2,1280]{2,1,0:T(2,128)(2,1)} %reshape.343), calls=%async_computation.2 | async-start | bytes 1310720 | tf_op jit(solution)/shard_map/all_to_all | solution.py:132
  132.8 2.1 gather_fusion.2
  136.7 1.1 fusion.12
  137.7 16.7 %all-to-all-done.2 = bf16[128,2,1280]{2,1,0:T(2,128)(2,1)S(1)} async-done(((bf16[128,2,1280]{2,1,0:T(2,128)(2,1)}), bf16[128,2,1280]{2,1,0:T(2,128)(2,1)S(1)}, u32[]{:S(2)}, u32[]{:S(2)}) %all-to-all-start.2) | async-done | bytes 655392 | tf_op jit(solution)/shard_map/all_to_all | solution.py:132
  154.4 1.5 gather_fusion.1
  156.6 5.1 %fusion.2 = f32[128,1280]{0,1:T(8,128)} fusion(bf16[1,1280,1280]{2,0,1:T(2,128)(2,1)} %all-gather.6.cloned.1.call-done, bf16[128,1,1280]{2,0,1:T(8,128)(2,1)S(1)} %copy-done.15, f32[1280]{0:T(1024)S(1)} %copy-done.26, f32[128]{0:T(128)S(1)} %add_rsqrt_fusion.1), kind=kOutput, calls=%fused_computation.12 | convolution fusion | flops 420085760 | bytes 4265472 | tf_op jit(solution)/shard_map/dot_general | solution.py:70
  161.7 34.2 %all-gather.4.cloned.1.call-done = bf16[3,1280,320]{2,0,1:T(4,128)(2,1)} async-done(((bf16[3,10,320]{2,0,1:T(4,128)(2,1)}), bf16[3,1280,320]{2,0,1:T(4,128)(2,1)}) %all-gather.4.cloned.1.call-update) | async-done | bytes 2457616 | tf_op jit(solution)/shard_map/all_gather | solution.py:116
  196.0 10.7 %fusion.59 = (bf16[1,1280,320]{2,0,1:T(2,128)(2,1)}, bf16[1,1280,320]{2,0,1:T(2,128)(2,1)}, bf16[1,1280,320]{2,0,1:T(2,128)(2,1)S(1)}) fusion(bf16[3,1280,320]{2,0,1:T(4,128)(2,1)} %all-gather.4.cloned.1.call-done), kind=kLoop, calls=%fused_computation.111 | loop fusion | bytes 4915200 | tf_op jit(solution)/shard_map/slice | solution.py:135
  206.7 3.9 %copy.63 = bf16[1,1280,320]{1,2,0:T(8,128)(2,1)S(1)} copy(bf16[1,1280,320]{2,0,1:T(2,128)(2,1)} %get-tuple-element.9) | data formatting | bytes 1638400
  210.6 10.2 %reduce-scatter.3.cloned.1.call-done = f32[128,320]{0,1:T(8,128)} async-done(((f32[128,1280]{0,1:T(8,128)}), f32[128,320]{0,1:T(8,128)}) %reduce-scatter.3.cloned.1.call-update) | async-done | bytes 163856 | tf_op jit(solution)/shard_map/reduce_scatter | solution.py:75
  220.8 1.6 convert_element_type.94
  222.3 1.0 copy.50
  224.1 15.1 %scatter_fusion.2 = bf16[128,2,320]{2,1,0:T(2,128)(2,1)} fusion(bf16[128,2,320]{2,1,0:T(2,128)(2,1)} %broadcast_in_dim.29, s32[128]{0:T(128)S(1)} %fusion.50, bf16[128,320]{1,0:T(8,128)(2,1)S(1)} %copy.50), kind=kCustom, calls=%fused_computation.5 | custom fusion | bytes 246784 | tf_op jit(solution)/shard_map/scatter | solution.py:85
  239.2 16.6 %all-to-all-start.3 = ((bf16[128,2,320]{2,1,0:T(2,128)(2,1)}), bf16[128,2,320]{2,1,0:T(2,128)(2,1)}, u32[]{:S(2)}, u32[]{:S(2)}) async-start(bf16[128,2,320]{2,1,0:T(2,128)(2,1)} %scatter_fusion.2), calls=%async_computation.4 | async-start | bytes 393216 | tf_op jit(solution)/shard_map/all_to_all | solution.py:88
  255.9 2.1 convolution_convert_fusion.4
  257.9 1.0 copy.57
  258.9 4.9 %copy.62 = bf16[1,1280,320]{1,2,0:T(8,128)(2,1)} copy(bf16[1,1280,320]{2,0,1:T(2,128)(2,1)} %get-tuple-element.10) | data formatting | bytes 1638400
  263.8 2.8 copy.61
  266.6 1.7 convolution_convert_fusion.5
  268.5 3.5 %scatter_fusion.3 = bf16[1280,320]{1,0:T(8,128)(2,1)} fusion(bf16[1280,320]{1,0:T(8,128)(2,1)} %bitcast.91, s32[128]{0:T(128)} %fusion.48, bf16[128,320]{1,0:T(8,128)(2,1)S(1)} %copy.57), kind=kCustom, calls=%fused_computation.6 | custom fusion | bytes 246272 | tf_op jit(solution)/shard_map/scatter | solution.py:141
  272.0 1.6 scatter_fusion.1
  273.7 1.1 reshape.336
  274.9 10.2 %all_gather.14 = bf16[256,1280]{0,1:T(8,128)(2,1)S(1)} all-gather(bf16[256,320]{0,1:T(8,128)(2,1)S(1)} %copy.51), channel_id=1, replica_groups=mesh['req'=128,'mlp'=4] {'mlp'}, dimensions={1}, use_global_device_ids=true | all-gather | bytes 819200 | tf_op jit(solution)/shard_map/all_gather | solution.py:101
  286.2 1.1 convolution_convert_fusion.1
  287.3 1.1 convolution_convert_fusion.3
  288.4 1.1 copy.58
  289.5 1.1 pad_maximum_fusion.1
  290.6 2.4 copy.59
  293.0 2.2 convolution_convert_fusion.2
  295.5 1.4 copy.53
  297.0 3.7 %fusion.60 = f32[4,256]{1,0:T(4,128)S(1)} fusion(pred[256,1536]{1,0:T(8,128)(4,1)S(1)} %copy-done.14, bf16[256,4,80]{0,2,1:T(8,128)(2,1)} %bitcast.96, bf16[1536,4,80]{0,2,1:T(8,128)(2,1)} %bitcast.92), kind=kOutput, calls=%fused_computation.112 | convolution fusion | flops 257951232 | bytes 1544192 | tf_op jit(solution)/shard_map/sub | solution.py:35
  300.7 3.9 %fusion.13 = bf16[4,80,256]{2,1,0:T(8,128)(2,1)S(1)} fusion(bf16[1536,4,80]{0,2,1:T(8,128)(2,1)} %bitcast.94, f32[4,256]{1,0:T(4,128)S(1)} %fusion.60, pred[256,1536]{1,0:T(8,128)(4,1)S(1)} %copy-done.14, bf16[256,4,80]{0,2,1:T(8,128)(2,1)S(1)} %bitcast.97, bf16[1536,4,80]{0,2,1:T(8,128)(2,1)S(1)} %bitcast.93), kind=kOutput, calls=%fused_computation.29 | convolution fusion | flops 511265280 | bytes 2691072 | tf_op jit(solution)/shard_map/hqk,khd->qhd/dot_general | solution.py:37
  304.7 1.6 fusion.61
  306.3 31.5 %reduce-scatter.5.cloned.1.call-done = f32[256,320]{0,1:T(8,128)} async-done(((f32[256,1280]{0,1:T(8,128)}), f32[256,320]{0,1:T(8,128)}) %reduce-scatter.5.cloned.1.call-update) | async-done | bytes 327696 | tf_op jit(solution)/shard_map/reduce_scatter | solution.py:154
  337.8 1.7 convert_bitcast_fusion
  (114 shorter events, 14.0 us)
Async XLA Ops:
  6.5 126.3 %copy-start = (bf16[1,256,1280]{2,1,0:T(8,128)(2,1)S(1)}, bf16[1,256,1280]{2,1,0:T(8,128)(2,1)}, u32[]{:S(2)}) copy-start(bf16[1,256,1280]{2,1,0:T(8,128)(2,1)} %param.22) | copy-start | bytes 1966084
  6.5 79.9 %copy-start.20 = (s32[128,1]{0,1:T(1,128)S(1)}, s32[128,1]{0,1:T(1,128)}, u32[]{:S(2)}) copy-start(s32[128,1]{0,1:T(1,128)} %param.19) | copy-start | bytes 1540
  6.5 79.9 %copy-start.18 = (s32[1,128,1]{1,2,0:T(1,128)S(1)}, s32[1,128,1]{1,2,0:T(1,128)}, u32[]{:S(2)}) copy-start(s32[1,128,1]{1,2,0:T(1,128)} %param.29) | copy-start | bytes 1540
  6.5 79.4 %copy-start.27 = (s32[1,128]{1,0:T(1,128)S(1)}, s32[1,128]{1,0:T(1,128)}, u32[]{:S(2)}) copy-start(s32[1,128]{1,0:T(1,128)} %param.31) | copy-start | bytes 1540
  6.5 80.8 %copy-start.24 = (s32[1,128]{1,0:T(1,128)S(1)}, s32[1,128]{1,0:T(1,128)}, u32[]{:S(2)}) copy-start(s32[1,128]{1,0:T(1,128)} %param.30) | copy-start | bytes 1540
  6.5 87.9 %copy-start.12 = (bf16[1,1280,320]{1,2,0:T(8,128)(2,1)S(1)}, bf16[1,1280,320]{1,2,0:T(8,128)(2,1)}, u32[]{:S(2)}) copy-start(bf16[1,1280,320]{1,2,0:T(8,128)(2,1)} %param.26) | copy-start | bytes 2457604
  6.6 150.0 %all-gather.6.cloned.1.call-start = ((), (), s32[]{:S(2)}) async-start(), calls=%async_computation.7 | async-start | bytes 6604800 | tf_op jit(solution)/shard_map/all_gather | solution.py:72
  8.2 187.8 %all-gather.4.cloned.1.call-start = ((), (), s32[]{:S(2)}) async-start(), calls=%async_computation.6 | async-start | bytes 3962880 | tf_op jit(solution)/shard_map/all_gather | solution.py:116
  11.4 88.7 %all-to-all-start = ((s32[128,1,1]{2,1,0:T(1,128)}), s32[128,1,1]{2,1,0:T(1,128)S(1)}, u32[]{:S(2)}, u32[]{:S(2)}) async-start(s32[128,1,1]{2,1,0:T(1,128)} %copy.44), calls=%async_computation | async-start | bytes 131072 | tf_op jit(solution)/shard_map/all_to_all | solution.py:89
  96.4 25.1 %copy-start.1 = (bf16[128,1280]{1,0:T(8,128)(2,1)S(1)}, bf16[128,1280]{1,0:T(8,128)(2,1)}, u32[]{:S(2)}) copy-start(bf16[128,1280]{1,0:T(8,128)(2,1)} %param.28) | copy-start | bytes 983044
  100.1 21.2 %all-to-all-start.1 = ((s32[128,1,2]{2,1,0:T(1,128)}), s32[128,1,2]{2,1,0:T(1,128)S(1)}, u32[]{:S(2)}, u32[]{:S(2)}) async-start(s32[128,1,2]{2,1,0:T(1,128)} %copy.46), calls=%async_computation.1 | async-start | bytes 131072 | tf_op jit(solution)/shard_map/all_to_all | solution.py:131
  123.7 30.7 %all-to-all-start.2 = ((bf16[128,2,1280]{2,1,0:T(2,128)(2,1)}), bf16[128,2,1280]{2,1,0:T(2,128)(2,1)S(1)}, u32[]{:S(2)}, u32[]{:S(2)}) async-start(bf16[128,2,1280]{2,1,0:T(2,128)(2,1)} %reshape.343), calls=%async_computation.2 | async-start | bytes 1310720 | tf_op jit(solution)/shard_map/all_to_all | solution.py:132
  130.9 89.9 %reduce-scatter.3.cloned.1.call-start = ((), (), s32[]{:S(2)}) async-start(), calls=%async_computation.8 | async-start | bytes 819200 | tf_op jit(solution)/shard_map/reduce_scatter | solution.py:75
  134.9 21.7 %copy-start.15 = (bf16[128,1,1280]{2,0,1:T(8,128)(2,1)S(1)}, bf16[128,1,1280]{2,0,1:T(8,128)(2,1)}, u32[]{:S(2)}) copy-start(bf16[128,1,1280]{2,0,1:T(8,128)(2,1)} %param.16) | copy-start | bytes 983044
  134.9 21.7 %copy-start.26 = (f32[1280]{0:T(1024)S(1)}, f32[1280]{0:T(1024)}, u32[]{:S(2)}) copy-start(f32[1280]{0:T(1024)} %param.17) | copy-start | bytes 15364
  155.9 5.8 %copy-start.10 = (bf16[128,1280]{1,0:T(8,128)(2,1)}, bf16[128,1280]{1,0:T(8,128)(2,1)S(1)}, u32[]{:S(2)}) copy-start(bf16[128,1280]{1,0:T(8,128)(2,1)S(1)} %gather_fusion.1) | copy-start | bytes 983044
  206.7 49.2 %copy-start.17 = (f32[1280]{0:T(1024)S(1)}, f32[1280]{0:T(1024)}, u32[]{:S(2)}) copy-start(f32[1280]{0:T(1024)} %param.23) | copy-start | bytes 15364
  210.6 53.2 %copy-start.5 = (bf16[1,1280,320]{1,2,0:T(8,128)(2,1)}, bf16[1,1280,320]{1,2,0:T(8,128)(2,1)S(1)}, u32[]{:S(2)}) copy-start(bf16[1,1280,320]{1,2,0:T(8,128)(2,1)S(1)} %copy.63) | copy-start | bytes 2457604
  239.2 34.5 %all-to-all-start.3 = ((bf16[128,2,320]{2,1,0:T(2,128)(2,1)}), bf16[128,2,320]{2,1,0:T(2,128)(2,1)}, u32[]{:S(2)}, u32[]{:S(2)}) async-start(bf16[128,2,320]{2,1,0:T(2,128)(2,1)} %scatter_fusion.2), calls=%async_computation.4 | async-start | bytes 393216 | tf_op jit(solution)/shard_map/all_to_all | solution.py:88
  255.8 82.0 %reduce-scatter.5.cloned.1.call-start = ((), (), s32[]{:S(2)}) async-start(), calls=%async_computation.9 | async-start | bytes 1638400 | tf_op jit(solution)/shard_map/reduce_scatter | solution.py:154
  266.6 7.1 %copy-start.7 = (bf16[1,1280,320]{1,2,0:T(8,128)(2,1)}, bf16[1,1280,320]{1,2,0:T(8,128)(2,1)S(1)}, u32[]{:S(2)}) copy-start(bf16[1,1280,320]{1,2,0:T(8,128)(2,1)S(1)} %copy.61) | copy-start | bytes 2457604
  266.6 5.4 %copy-start.2 = (bf16[1,1280,320]{2,1,0:T(8,128)(2,1)S(1)}, bf16[1,1280,320]{2,1,0:T(8,128)(2,1)}, u32[]{:S(2)}) copy-start(bf16[1,1280,320]{2,1,0:T(8,128)(2,1)} %copy.45) | copy-start | bytes 2457604
  266.6 5.4 %copy-start.21 = (s32[128]{0:T(128)S(1)}, s32[128]{0:T(128)}, u32[]{:S(2)}) copy-start(s32[128]{0:T(128)} %fusion.48) | copy-start | bytes 1540
  268.5 16.6 %copy-start.9 = (bf16[256,1280]{1,0:T(8,128)(2,1)S(1)}, bf16[256,1280]{1,0:T(8,128)(2,1)}, u32[]{:S(2)}) copy-start(bf16[256,1280]{1,0:T(8,128)(2,1)} %gather_fusion.2) | copy-start | bytes 1966084
  272.0 13.1 %copy-start.19 = (s32[256]{0:T(256)S(1)}, s32[256]{0:T(256)}, u32[]{:S(2)}) copy-start(s32[256]{0:T(256)} %get-tuple-element.17) | copy-start | bytes 3076
  272.0 13.1 %copy-start.22 = (pred[256]{0:T(512)(128)(4,1)S(1)}, pred[256]{0:T(512)(128)(4,1)}, u32[]{:S(2)}) copy-start(pred[256]{0:T(512)(128)(4,1)} %get-tuple-element.14) | copy-start | bytes 772
  272.0 13.1 %copy-start.23 = (pred[256]{0:T(512)(128)(4,1)S(1)}, pred[256]{0:T(512)(128)(4,1)}, u32[]{:S(2)}) copy-start(pred[256]{0:T(512)(128)(4,1)} %get-tuple-element.15) | copy-start | bytes 772
  285.1 1.1 copy-start.6
  285.6 1.7 copy-start.8
  285.6 3.9 %copy-start.3 = (bf16[1280,320]{1,0:T(8,128)(2,1)S(1)}, bf16[1280,320]{1,0:T(8,128)(2,1)}, u32[]{:S(2)}) copy-start(bf16[1280,320]{1,0:T(8,128)(2,1)} %scatter_fusion.3) | copy-start | bytes 2457604
  290.6 4.6 %copy-start.13 = (bf16[256,320]{0,1:T(8,128)(2,1)S(1)}, bf16[256,320]{0,1:T(8,128)(2,1)}, u32[]{:S(2)}) copy-start(bf16[256,320]{0,1:T(8,128)(2,1)} %convolution_convert_fusion.3) | copy-start | bytes 491524
  295.2 1.7 copy-start.14
  297.0 3.7 %copy-start.11 = (bf16[1536,320]{0,1:T(8,128)(2,1)S(1)}, bf16[1536,320]{0,1:T(8,128)(2,1)}, u32[]{:S(2)}) copy-start(bf16[1536,320]{0,1:T(8,128)(2,1)} %copy.59) | copy-start | bytes 2949124
  297.0 3.8 %copy-start.16 = (bf16[256,320]{0,1:T(8,128)(2,1)S(1)}, bf16[256,320]{0,1:T(8,128)(2,1)}, u32[]{:S(2)}) copy-start(bf16[256,320]{0,1:T(8,128)(2,1)} %convolution_convert_fusion.2) | copy-start | bytes 491524
  300.7 4.0 %copy-start.25 = (pred[256]{0:T(512)(128)(4,1)S(1)}, pred[256]{0:T(512)(128)(4,1)}, u32[]{:S(2)}) copy-start(pred[256]{0:T(512)(128)(4,1)} %iota_compare_fusion.4) | copy-start | bytes 772
  300.7 4.0 %copy-start.4 = (bf16[1280,320]{1,0:T(8,128)(2,1)S(1)}, bf16[1280,320]{1,0:T(8,128)(2,1)}, u32[]{:S(2)}) copy-start(bf16[1280,320]{1,0:T(8,128)(2,1)} %reshape.394) | copy-start | bytes 2457604
Sparse Core Ops, SparseCore 0:
  10.6 93.5 all-gather.5
  107.3 88.5 all-gather.3
  198.8 21.9 reduce-scatter.2
  306.4 31.3 reduce-scatter.4
where the time goes:
time: 348 us; the launch traced here: 346 us
  waiting for transfers between devices  100 us (29%)
  local copies, waits for them, and re-layouts  73.3 us (21%)
  blocking collectives  63.4 us (18%)
  starting transfers between devices  52 us (15%)
  matrix products  23 us (7%)
  other arithmetic  17.4 us (5%)
  between operations  16.9 us (5%)
    all_gather x1, blocking collectives, local(): lax.all_gather(out_weight, 'req', axis=1, tiled=True)  53.2 us
    all_gather x1, waiting for transfers between devices, local(): weight_cols = lax.all_gather(qkv_weight, 'req', axis=1, tiled=True)  34.2 us
    reduce_scatter x1, waiting for transfers between devices, local(): lax.psum_scatter(terms, 'mlp', scatter_dimension=1, tiled=True)  31.5 us
    unnamed x63, local copies, waits for them, and re-layouts  18.6 us
    all_to_all x1, starting transfers between devices, local(): lax.all_to_all(image_counts.reshape(n_req, 1), 'req', split_axis=0, conca...  18.4 us
    all_to_all x1, waiting for transfers between devices, local(): lax.all_to_all(picked, 'req', split_axis=0, concat_axis=0, tiled=True)  16.7 us
    all_to_all x1, starting transfers between devices, local(): lax.all_to_all(outgoing, 'req', split_axis=0, concat_axis=0, tiled=True)  16.6 us
    scatter x1, local copies, waits for them, and re-layouts, local(): outgoing = jnp.zeros((n_req, capacity, image_tokens.shape[1]), jnp.bfloat...  15.1 us
  transfers between devices with their start and end apart: 8, of which 5 were waited for; matrix products, arithmetic and copies ran while one was open for 20% of the time, Pallas kernels for 0%

commit v1 on v0

v1 whole, which is shorter than its diff:
```python
import functools

import jax
import jax.numpy as jnp
import numpy as np
from jax import lax
from jax.experimental import pallas as pl
from jax.experimental.pallas import tpu as pltpu
from jax.sharding import PartitionSpec as P

HEAD_DIM = 80
eps = 1e-06
big_negative = -1e30
MESH = pl.DeviceIdType.MESH
NZ, NY, NC, NX = 8, 8, 2, 4
GROUP = NY * NC
WIDTH = 1280
HALF = WIDTH // 2
SHARD = 10
PIECE = 16
BLOCK = GROUP * SHARD
WINDOW = 384
OFFSETS = (0, 256, 640, 896)
WIDTHS = (256, 384, 256, 384)
ROWS = 256
HEADS = 4
LOCAL = HEADS * HEAD_DIM
f32, bf16 = jnp.float32, jnp.bfloat16


def coords():
    r, m = lax.axis_index("req"), lax.axis_index("mlp")
    return r, m, lax.div(r, GROUP), lax.rem(lax.div(r, NC), NY), lax.rem(r, NC)


def at(z, y, c, m):
    return (z * GROUP + y * NC + c, m)


def send(src, dst, send_sem, recv_sem, device):
    copy = pltpu.make_async_remote_copy(
        src_ref=src,
        dst_ref=dst,
        send_sem=send_sem,
        recv_sem=recv_sem,
        device_id=device,
        device_id_type=MESH,
    )
    copy.start()
    return copy


def arrival(dst, send_sem, recv_sem, device):
    pltpu.make_async_remote_copy(
        src_ref=dst,
        dst_ref=dst,
        send_sem=send_sem,
        recv_sem=recv_sem,
        device_id=device,
        device_id_type=MESH,
    ).wait_recv()


def meet(devices):
    barrier = pltpu.get_barrier_semaphore()
    for device in devices:
        pl.semaphore_signal(barrier, inc=1, device_id=device, device_id_type=MESH)
    pl.semaphore_wait(barrier, len(devices))


def iota(shape, dim):
    return lax.broadcasted_iota(jnp.int32, shape, dim)


def hot(mask):
    return jnp.where(mask, 1.0, 0.0).astype(bf16)


def mm(a, b):
    return jnp.dot(a, b, preferred_element_type=f32)


def mm_t(a, b):
    return lax.dot_general(a, b, (((1,), (1,)), ((), ())), preferred_element_type=f32)


def norm(x, gain):
    scale = lax.rsqrt(jnp.mean(x * x, -1, keepdims=True) + eps)
    return (x * scale * gain).astype(bf16)


def swap_order(rows_first):
    a, b = iota((ROWS, ROWS), 0), iota((ROWS, ROWS), 1)
    if not rows_first:
        a, b = b, a
    other = (a & 7) * 32 + ((a >> 3) & 1) * 16 + (a >> 4)
    return hot(other == b)


class Ring:
    def __init__(self, out, own, half, place, right, left, sibling, sems):
        self.out, self.own, self.half, self.place = out, own, half, place
        self.right, self.left, self.sibling = right, left, sibling
        self.ssem, self.rsem, self.local = sems
        self.sent = []

    def spot(self, half, number, part=None):
        ref = self.out.at[half, lax.rem(number + 2 * NZ, NZ)]
        if part is None:
            return ref
        return ref.at[pl.ds(part * (BLOCK // 2), BLOCK // 2)]

    def push(self, src, dst, slot, device):
        self.sent.append(send(src, dst, self.ssem.at[slot], self.rsem.at[slot], device))

    def start(self):
        dst = self.spot(self.half, self.place)
        self.push(self.own, dst, 0, self.right)
        self.push(self.own, dst, 4, self.left)
        self.push(self.own, dst, 8, self.sibling)
        self.kept = pltpu.make_async_copy(self.own, dst, self.local)
        self.kept.start()

    def step(self, s):
        for side, sign, device, base in ((0, -1, self.right, 0), (1, 1, self.left, 4)):
            number = self.place + sign * (1 + s)
            part = side if s == 3 else None
            got = self.spot(self.half, number, part)
            arrival(got, self.ssem.at[base + s], self.rsem.at[base + s], device)
            if s < 3:
                onward = self.spot(self.half, number, side if s == 2 else None)
                self.push(onward, onward, base + s + 1, device)
            self.push(got, got, 9 + 2 * s + side, self.sibling)

    def finish(self):
        other = 1 - self.half
        slot = 8
        arrival(self.spot(other, self.place), self.ssem.at[slot], self.rsem.at[slot], self.sibling)
        for s in range(4):
            for side, sign in ((0, -1), (1, 1)):
                slot = 9 + 2 * s + side
                got = self.spot(other, self.place + sign * (1 + s), side if s == 3 else None)
                arrival(got, self.ssem.at[slot], self.rsem.at[slot], self.sibling)
        self.kept.wait()


def gather_kernel(
    wa_ref,
    wb_ref,
    idx_ref,
    held_ref,
    dense_ref,
    full_a,
    full_b,
    out_cols,
    held_out,
    table,
    piece_a,
    piece_b,
    stage_a,
    stage_b,
    own_a,
    own_b,
    idx_stage,
    idx_own,
    picked,
    hop,
    turned,
    sem_as,
    sem_ar,
    sem_bs,
    sem_br,
    sem_is,
    sem_ir,
    sem_ts,
    sem_tr,
    sem_hs,
    sem_hr,
    sem_gs,
    sem_gr,
    sem_xs,
    sem_xr,
    sem_ras,
    sem_rar,
    sem_rbs,
    sem_rbr,
    sem_local,
):
    r, m, z, y, c = coords()
    yc = y * NC + c
    sibling = at(z, y, 1 - c, m)
    planes = [(r, lax.rem(m + d, NX)) for d in range(1, NX)]
    turn_y = [lax.rem(y + d, NY) for d in range(NY)]
    turn_z = [lax.rem(z + d, NZ) for d in range(NZ)]
    back_y = [lax.rem(y + NY - d, NY) for d in range(NY)]
    back_z = [lax.rem(z + NZ - d, NZ) for d in range(NZ)]
    peers = [sibling] + planes
    peers += [at(z, turn_y[d], h, m) for d in range(1, NY) for h in range(NC)]
    peers += [at(turn_z[d], y, h, m) for d in range(1, NZ) for h in range(NC)]
    meet(peers)
    sent = []

    idx_stage[pl.ds(pl.multiple_of(z * 8, 8), 8), :] = idx_ref[...]
    for d in range(1, NZ):
        dst = idx_stage.at[pl.ds(pl.multiple_of(z * 8, 8), 8)]
        sent.append(send(idx_ref, dst, sem_is.at[d], sem_ir.at[d], at(turn_z[d], y, c, m)))

    for piece, ref in ((piece_a, wa_ref), (piece_b, wb_ref)):
        for h in range(NC):
            piece[h] = jnp.zeros((PIECE, HALF), bf16)
            piece[h, 0:SHARD, :] = ref[:, h * HALF : (h + 1) * HALF]

    stage_a[z * NC + c] = jnp.where(c == 0, piece_a[0].astype(f32), piece_a[1].astype(f32)).astype(bf16)
    stage_b[yc] = jnp.where(c == 0, piece_b[0].astype(f32), piece_b[1].astype(f32)).astype(bf16)
    spot_a, spot_b = stage_a.at[z * NC + c], stage_b.at[yc]
    sent.append(send(piece_a.at[1 - c], spot_a, sem_as.at[0, 0], sem_ar.at[0, 0], sibling))
    sent.append(send(piece_b.at[1 - c], spot_b, sem_bs.at[0, 0], sem_br.at[0, 0], sibling))
    for d in range(1, NZ):
        for k in range(NC):
            h = c if k == 0 else 1 - c
            sent.append(
                send(piece_a.at[h], spot_a, sem_as.at[d, k], sem_ar.at[d, k], at(turn_z[d], y, h, m))
            )
            sent.append(
                send(piece_b.at[h], spot_b, sem_bs.at[d, k], sem_br.at[d, k], at(z, turn_y[d], h, m))
            )

    for d in range(1, NZ):
        got = idx_stage.at[pl.ds(pl.multiple_of(back_z[d] * 8, 8), 8)]
        arrival(got, sem_is.at[d], sem_ir.at[d], at(back_z[d], y, c, m))
    for which in range(2):
        idx_own[which] = idx_stage[pl.ds(which, NZ, stride=8), :]
    table[yc] = idx_own[...]
    sent.append(send(idx_own, table.at[yc], sem_ts.at[0, 0], sem_tr.at[0, 0], sibling))
    for d in range(1, NY):
        for k in range(NC):
            h = c if k == 0 else 1 - c
            sent.append(
                send(idx_own, table.at[yc], sem_ts.at[d, k], sem_tr.at[d, k], at(z, turn_y[d], h, m))
            )

    ring_a = Ring(
        full_a, own_a, c, y, at(z, turn_y[1], c, m), at(z, back_y[1], c, m), sibling,
        (sem_ras, sem_rar, sem_local.at[0]),
    )
    ring_b = Ring(
        full_b, own_b, c, z, at(turn_z[1], y, c, m), at(back_z[1], y, c, m), sibling,
        (sem_rbs, sem_rbr, sem_local.at[1]),
    )
    arrival(stage_a.at[z * NC + 1 - c], sem_as.at[0, 0], sem_ar.at[0, 0], sibling)
    for d in range(1, NZ):
        for k in range(NC):
            h = c if k == 0 else 1 - c
            arrival(stage_a.at[back_z[d] * NC + h], sem_as.at[d, k], sem_ar.at[d, k], at(back_z[d], y, h, m))
    own_a[...] = mm(dense_ref[...], stage_a[...].reshape(GROUP * PIECE, HALF)).astype(bf16)
    ring_a.start()
    arrival(stage_b.at[y * NC + 1 - c], sem_bs.at[0, 0], sem_br.at[0, 0], sibling)
    for d in range(1, NY):
        for k in range(NC):
            h = c if k == 0 else 1 - c
            arrival(stage_b.at[back_y[d] * NC + h], sem_bs.at[d, k], sem_br.at[d, k], at(z, back_y[d], h, m))
    own_b[...] = mm(dense_ref[...], stage_b[...].reshape(GROUP * PIECE, HALF)).astype(bf16)
    ring_b.start()

    arrival(table.at[y * NC + 1 - c], sem_ts.at[0, 0], sem_tr.at[0, 0], sibling)
    for d in range(1, NY):
        for k in range(NC):
            h = c if k == 0 else 1 - c
            arrival(table.at[back_y[d] * NC + h], sem_ts.at[d, k], sem_tr.at[d, k], at(z, back_y[d], h, m))
    code = table[:, 1]
    mine = (code >> 7) == r
    row = (code & 127).astype(f32)
    lane = iota((GROUP, NZ, 128), 2).astype(f32)
    first = jnp.min(jnp.where(mine, lane, 1000.0), -1, keepdims=True)
    is_first = mine & (lane == first)
    want0 = jnp.sum(jnp.where(is_first, row, 0.0), -1, keepdims=True)
    want1 = jnp.sum(jnp.where(mine, row, 0.0), -1, keepdims=True) - want0
    pick0 = jnp.where(lane == want0, 1.0, 0.0)
    pick1 = jnp.where(lane == want1, 1.0, 0.0)
    pick = jnp.concatenate([pick0, pick1], 1).reshape(ROWS, 128).astype(bf16)
    base = pl.multiple_of(m * 320 - lax.rem(m, 2) * 64, 128)
    picked[...] = mm(pick, held_ref[:, pl.ds(base, WINDOW)]).astype(bf16).reshape(GROUP, 16, WINDOW)
    hop[yc] = picked[yc]
    sent.append(
        send(picked.at[y * NC + 1 - c], hop.at[yc], sem_hs.at[0, 0], sem_hr.at[0, 0], sibling)
    )
    for d in range(1, NY):
        for k in range(NC):
            h = c if k == 0 else 1 - c
            sent.append(
                send(
                    picked.at[turn_y[d] * NC + h], hop.at[yc], sem_hs.at[d, k], sem_hr.at[d, k],
                    at(z, turn_y[d], h, m),
                )
            )

    ring_a.step(0)
    ring_b.step(0)

    arrival(hop.at[y * NC + 1 - c], sem_hs.at[0, 0], sem_hr.at[0, 0], sibling)
    for d in range(1, NY):
        for k in range(NC):
            h = c if k == 0 else 1 - c
            arrival(hop.at[back_y[d] * NC + h], sem_hs.at[d, k], sem_hr.at[d, k], at(z, back_y[d], h, m))
    back = mm(swap_order(False), hop[...].reshape(ROWS, WINDOW)).astype(bf16)
    turned[...] = back.reshape(NZ, 32, WINDOW)
    keep = pltpu.make_async_copy(turned.at[z], held_out.at[m, z], sem_local.at[2])
    keep.start()
    for d in range(1, NZ):
        sent.append(
            send(
                turned.at[turn_z[d]], held_out.at[m, z], sem_gs.at[d], sem_gr.at[d],
                at(turn_z[d], y, c, m),
            )
        )

    ring_a.step(1)
    ring_b.step(1)

    keep.wait()
    for d in range(1, NZ):
        arrival(held_out.at[m, back_z[d]], sem_gs.at[d], sem_gr.at[d], at(back_z[d], y, c, m))
    for d in range(1, NX):
        sent.append(send(held_out.at[m], held_out.at[m], sem_xs.at[0, d], sem_xr.at[0, d], planes[d - 1]))

    for s in range(2, 4):
        ring_a.step(s)
        ring_b.step(s)
    ring_b.finish()

    def columns(plane):
        return full_b.at[1, pl.ds(plane * 2, 2), :, pl.ds(0, WINDOW)]

    for d in range(1, NX):
        other = lax.rem(m + d, NX)
        sent.append(send(columns(other), out_cols.at[m], sem_xs.at[1, d], sem_xr.at[1, d], planes[d - 1]))
    mine_cols = pltpu.make_async_copy(columns(m), out_cols.at[m], sem_local.at[3])
    mine_cols.start()
    ring_a.finish()
    mine_cols.wait()
    for d in range(1, NX):
        other = lax.rem(m + NX - d, NX)
        arrival(held_out.at[other], sem_xs.at[0, d], sem_xr.at[0, d], (r, other))
        arrival(out_cols.at[other], sem_xs.at[1, d], sem_xr.at[1, d], (r, other))
    for copy in sent + ring_a.sent + ring_b.sent:
        copy.wait_send()


def image_kernel(
    patch_ref,
    gain_ref,
    weight_ref,
    dest_col,
    dest_row,
    out,
    part,
    parts,
    picked,
    hop,
    turned,
    sem_ps,
    sem_pr,
    sem_zs,
    sem_zr,
    sem_ys,
    sem_yr,
    sem_xs,
    sem_xr,
):
    r, m, z, y, c = coords()
    yc = y * NC + c
    sibling = at(z, y, 1 - c, m)
    planes = [(r, lax.rem(m + d, NX)) for d in range(1, NX)]
    turn_y = [lax.rem(y + d, NY) for d in range(NY)]
    turn_z = [lax.rem(z + d, NZ) for d in range(NZ)]
    back_y = [lax.rem(y + NY - d, NY) for d in range(NY)]
    back_z = [lax.rem(z + NZ - d, NZ) for d in range(NZ)]
    peers = [sibling] + planes
    peers += [at(z, turn_y[d], h, m) for d in range(1, NY) for h in range(NC)]
    peers += [at(turn_z[d], y, c, m) for d in range(1, NZ)]
    meet(peers)
    sent = []

    normed = norm(patch_ref[...].astype(f32), gain_ref[...])
    k, j = iota((WIDTH, WIDTH), 0), iota((WIDTH, WIDTH), 1)
    jz, jy, ji = lax.div(lax.rem(j, 160), 20), lax.div(j, 160), lax.rem(j, 20)
    order = hot(k == jz * 160 + jy * 20 + ji)
    normed = mm(normed, order).astype(bf16)
    left = mm(normed, weight_ref[0].reshape(WIDTH, HALF))
    right = mm(normed, weight_ref[1].reshape(WIDTH, HALF))
    part[0] = left[:, 0:384]
    part[1] = left[:, 256:640]
    part[2] = right[:, 0:384]
    part[3] = right[:, 256:640]
    for d in range(1, NX):
        other = lax.rem(m + d, NX)
        sent.append(send(part.at[other], parts.at[m], sem_ps.at[d], sem_pr.at[d], planes[d - 1]))

    before = (dest_col[...] == dest_row[...]) & (iota((128, 128), 0) < iota((128, 128), 1))
    rank = jnp.sum(jnp.where(before, 1.0, 0.0), 0, keepdims=True)
    q = iota((ROWS, 128), 0)
    target = (q >> 5) * 16 + (q & 15)
    slot = ((q >> 4) & 1).astype(f32)
    choose = hot((dest_row[...] == target) & (rank == slot))
    turn = swap_order(True)

    total = part[m]
    for d in range(1, NX):
        other = lax.rem(m + NX - d, NX)
        arrival(parts.at[other], sem_ps.at[d], sem_pr.at[d], (r, other))
    for d in range(1, NX):
        total = total + parts[lax.rem(m + NX - d, NX)]
    tokens = total.astype(bf16)
    picked[...] = mm(choose, tokens).astype(bf16).reshape(NZ, 32, WINDOW)
    hop[z] = picked[z]
    for d in range(1, NZ):
        sent.append(
            send(picked.at[turn_z[d]], hop.at[z], sem_zs.at[d], sem_zr.at[d], at(turn_z[d], y, c, m))
        )
    for d in range(1, NZ):
        arrival(hop.at[back_z[d]], sem_zs.at[d], sem_zr.at[d], at(back_z[d], y, c, m))
    turned[...] = mm(turn, hop[...].reshape(ROWS, WINDOW)).astype(bf16).reshape(GROUP, 16, WINDOW)
    out[m, yc] = turned[yc]
    sent.append(
        send(turned.at[y * NC + 1 - c], out.at[m, yc], sem_ys.at[0, 0], sem_yr.at[0, 0], sibling)
    )
    for d in range(1, NY):
        for k in range(NC):
            h = c if k == 0 else 1 - c
            sent.append(
                send(
                    turned.at[turn_y[d] * NC + h], out.at[m, yc], sem_ys.at[d, k], sem_yr.at[d, k],
                    at(z, turn_y[d], h, m),
                )
            )
    arrival(out.at[m, y * NC + 1 - c], sem_ys.at[0, 0], sem_yr.at[0, 0], sibling)
    for d in range(1, NY):
        for k in range(NC):
            h = c if k == 0 else 1 - c
            arrival(out.at[m, back_y[d] * NC + h], sem_ys.at[d, k], sem_yr.at[d, k], at(z, back_y[d], h, m))
    for d in range(1, NX):
        sent.append(send(out.at[m], out.at[m], sem_xs.at[d], sem_xr.at[d], planes[d - 1]))
    for d in range(1, NX):
        other = lax.rem(m + NX - d, NX)
        arrival(out.at[other], sem_xs.at[d], sem_xr.at[d], (r, other))
    for copy in sent:
        copy.wait_send()


def attend_kernel(
    scalars,
    image_ref,
    held_ref,
    table,
    text_ref,
    gain_ref,
    weight_ref,
    out_cols,
    cache_keys,
    cache_values,
    owner_col,
    owner_row,
    place_row,
    result,
    rows,
    normed,
    keys,
    values,
    mixed_all,
    sem_s,
    sem_r,
):
    r, m, z, y, c = coords()
    planes = [(r, lax.rem(m + d, NX)) for d in range(1, NX)]
    meet(planes)

    mine = hot(table[:, 0].reshape(128, 128) == r)
    counts = mm_t(jnp.ones((8, 128), bf16), mine)
    s0, s1 = iota((128, 128), 0), iota((128, 128), 1)
    earlier = hot((s0 & 7) * 16 + (s0 >> 3) < (s1 & 7) * 16 + (s1 >> 3))
    before = mm(counts.astype(bf16), earlier)
    s, a = iota((128, ROWS), 0), iota((128, ROWS), 1)
    spread = hot(((s >> 3) == (a >> 4)) & ((s & 7) == (a & 7)))
    counts_a = mm(counts.astype(bf16), spread)[0:1]
    before_a = mm(before.astype(bf16), spread)[0:1]
    slot = ((iota((1, ROWS), 1) >> 3) & 1).astype(f32)
    number = jnp.sum(counts[0:1], -1, keepdims=True)
    asked = jnp.full((1, 1), scalars[0], jnp.int32).astype(f32)
    text_len = jnp.full((1, 1), scalars[1], jnp.int32).astype(f32)
    start = jnp.minimum(asked, ROWS - number)
    length = jnp.minimum(float(ROWS), text_len + number)
    q = iota((ROWS, ROWS), 0).astype(f32)
    t = iota((ROWS, ROWS), 1).astype(f32)
    choose = hot((before_a + slot == q - start) & (counts_a > slot))
    take = hot(((q < start) & (t == q)) | ((q >= start + number) & (t == q - number)))
    for b in range(NX):
        o, w = OFFSETS[b], WIDTHS[b]
        image = image_ref[b].reshape(ROWS, WINDOW)[:, 0:w]
        rows[0:ROWS, o : o + w] = mm(choose, image) + mm(take, text_ref[:, o : o + w])

    same = (owner_col[...] == owner_row[...]) & (iota((128, 128), 1) < iota((128, 128), 0))
    rank = jnp.sum(jnp.where(same, 1.0, 0.0), -1, keepdims=True).astype(jnp.int32)
    owner = owner_col[...]
    spot = (owner >> 4) * 32 + rank * 16 + (owner & 15)
    fetch = hot(spot == iota((128, ROWS), 1))
    for b in range(NX):
        o, w = OFFSETS[b], WIDTHS[b]
        held = held_ref[b].reshape(ROWS, WINDOW)[:, 0:w]
        rows[ROWS : ROWS + 128, o : o + w] = mm(fetch, held)
    normed[...] = norm(rows[...], gain_ref[...])

    first = weight_ref[0].reshape(WIDTH, HALF)
    second = weight_ref[1].reshape(WIDTH, HALF)
    queries = mm(normed[0:ROWS], first[:, 0:384]).astype(bf16)[:, 0:LOCAL]
    fresh_k = mm(normed[...], first[:, 256:640]).astype(bf16)[:, 64:384]
    fresh_v = mm(normed[...], second[:, 256:640]).astype(bf16)[:, 64:384]
    keys[WIDTH:, :] = fresh_k[0:ROWS]
    values[WIDTH:, :] = fresh_v[0:ROWS]
    fresh_k, fresh_v = fresh_k[ROWS:], fresh_v[ROWS:]
    for b in range(5):
        span = slice(b * 256, (b + 1) * 256)
        match = place_row[...] == iota((256, 128), 0) + b * 256
        put = hot(match)
        hit = jnp.sum(jnp.where(match, 1.0, 0.0), -1, keepdims=True) > 0.0
        keys[span, :] = jnp.where(hit, mm(put, fresh_k), cache_keys[span, :].astype(f32)).astype(bf16)
        values[span, :] = jnp.where(hit, mm(put, fresh_v), cache_values[span, :].astype(f32)).astype(bf16)

    lanes = iota((ROWS, LOCAL), 1)
    seen = (t <= q) & (t < length)
    mixed = jnp.zeros((ROWS, LOCAL), f32)
    for h in range(HEADS):
        inside = (lanes >= h * HEAD_DIM) & (lanes < (h + 1) * HEAD_DIM)
        part = jnp.where(inside, queries.astype(f32), 0.0).astype(bf16)
        scores = mm_t(part, keys[...]) * HEAD_DIM ** (-0.5)
        old, new = scores[:, 0:WIDTH], jnp.where(seen, scores[:, WIDTH:], big_negative)
        highest = jnp.maximum(jnp.max(old, -1, keepdims=True), jnp.max(new, -1, keepdims=True))
        old, new = jnp.exp(old - highest), jnp.exp(new - highest)
        inverse = 1.0 / (jnp.sum(old, -1, keepdims=True) + jnp.sum(new, -1, keepdims=True))
        old, new = (old * inverse).astype(bf16), (new * inverse).astype(bf16)
        summed = mm(old, values[0:WIDTH]) + mm(new, values[WIDTH:])
        mixed = jnp.where(inside, summed, mixed)
    mixed = jnp.where(iota((ROWS, LOCAL), 0).astype(f32) < length, mixed, 0.0)
    mixed_all[m] = mixed.astype(bf16)

    sent = []
    for d in range(1, NX):
        sent.append(send(mixed_all.at[m], mixed_all.at[m], sem_s.at[d], sem_r.at[d], planes[d - 1]))
    terms = mm_t(mixed_all[m], out_cols[m].reshape(LOCAL, WINDOW)[:, 0:LOCAL])
    for d in range(1, NX):
        other = lax.rem(m + NX - d, NX)
        arrival(mixed_all.at[other], sem_s.at[d], sem_r.at[d], (r, other))
        terms = terms + mm_t(mixed_all[other], out_cols[other].reshape(LOCAL, WINDOW)[:, 0:LOCAL])
    result[...] = terms.astype(bf16)
    for copy in sent:
        copy.wait_send()


VM = functools.partial(pl.BlockSpec, memory_space=pltpu.VMEM)
HB = functools.partial(pl.BlockSpec, memory_space=pl.ANY)
SD = jax.ShapeDtypeStruct
DMA = pltpu.SemaphoreType.DMA


def params(number):
    return pltpu.CompilerParams(
        collective_id=number, has_side_effects=True, vmem_limit_bytes=48 * 1024 * 1024
    )


def local(
    patches,
    vis_gain,
    proj_weight,
    image_dest,
    image_pos,
    text_len,
    text,
    attn_gain,
    qkv_weight,
    out_weight,
    cache_keys,
    cache_values,
    held,
    held_owner,
    held_row,
    recompute_pos,
):
    wb = jnp.concatenate([qkv_weight[0], qkv_weight[1], out_weight.T, qkv_weight[2]], 1)
    dest_row = image_dest.reshape(1, 128)
    owner_row = held_owner.reshape(1, 128)
    idx = jnp.concatenate([dest_row, owner_row * 128 + held_row, jnp.zeros((6, 128), jnp.int32)], 0)
    k, p = np.arange(BLOCK)[:, None], np.arange(GROUP * PIECE)[None, :]
    dense = jnp.asarray((p == k // SHARD * PIECE + k % SHARD).astype(np.float32)).astype(bf16)

    full_a, full_b, out_cols, held_rows, table = pl.pallas_call(
        gather_kernel,
        out_shape=(
            SD((2, NY, BLOCK, HALF), bf16),
            SD((2, NZ, BLOCK, HALF), bf16),
            SD((NX, 2, BLOCK, WINDOW), bf16),
            SD((NX, NZ, 32, WINDOW), bf16),
            SD((GROUP, 2, NZ, 128), jnp.int32),
        ),
        in_specs=[VM()] * 5,
        out_specs=(HB(), HB(), HB(), HB(), VM()),
        scratch_shapes=[
            pltpu.VMEM((2, PIECE, HALF), bf16),
            pltpu.VMEM((2, PIECE, HALF), bf16),
            pltpu.VMEM((GROUP, PIECE, HALF), bf16),
            pltpu.VMEM((GROUP, PIECE, HALF), bf16),
            pltpu.VMEM((BLOCK, HALF), bf16),
            pltpu.VMEM((BLOCK, HALF), bf16),
            pltpu.VMEM((64, 128), jnp.int32),
            pltpu.VMEM((2, NZ, 128), jnp.int32),
            pltpu.VMEM((GROUP, 16, WINDOW), bf16),
            pltpu.VMEM((GROUP, 16, WINDOW), bf16),
            pltpu.VMEM((NZ, 32, WINDOW), bf16),
            DMA((NZ, 2)),
            DMA((NZ, 2)),
            DMA((NY, 2)),
            DMA((NY, 2)),
            DMA((NZ,)),
            DMA((NZ,)),
            DMA((NY, 2)),
            DMA((NY, 2)),
            DMA((NY, 2)),
            DMA((NY, 2)),
            DMA((NZ,)),
            DMA((NZ,)),
            DMA((2, NX)),
            DMA((2, NX)),
            DMA((17,)),
            DMA((17,)),
            DMA((17,)),
            DMA((17,)),
            DMA((4,)),
        ],
        compiler_params=params(1),
    )(proj_weight[0], wb, idx, held, dense)

    image_rows = pl.pallas_call(
        image_kernel,
        out_shape=SD((NX, GROUP, 16, WINDOW), bf16),
        in_specs=[VM()] * 5,
        out_specs=VM(),
        scratch_shapes=[
            pltpu.VMEM((NX, 128, WINDOW), f32),
            pltpu.VMEM((NX, 128, WINDOW), f32),
            pltpu.VMEM((NZ, 32, WINDOW), bf16),
            pltpu.VMEM((NZ, 32, WINDOW), bf16),
            pltpu.VMEM((GROUP, 16, WINDOW), bf16),
            DMA((NX,)),
            DMA((NX,)),
            DMA((NZ,)),
            DMA((NZ,)),
            DMA((NY, 2)),
            DMA((NY, 2)),
            DMA((NX,)),
            DMA((NX,)),
        ],
        compiler_params=params(2),
    )(patches[:, 0], vis_gain[None], full_a, image_dest, dest_row)

    scalars = jnp.concatenate([image_pos, text_len])
    result = pl.pallas_call(
        attend_kernel,
        out_shape=SD((ROWS, LOCAL), bf16),
        in_specs=[pl.BlockSpec(memory_space=pltpu.SMEM)] + [VM()] * 12,
        out_specs=VM(),
        scratch_shapes=[
            pltpu.VMEM((ROWS + 128, WIDTH), f32),
            pltpu.VMEM((ROWS + 128, WIDTH), bf16),
            pltpu.VMEM((WIDTH + ROWS, LOCAL), bf16),
            pltpu.VMEM((WIDTH + ROWS, LOCAL), bf16),
            pltpu.VMEM((NX, ROWS, LOCAL), bf16),
            DMA((NX,)),
            DMA((NX,)),
        ],
        compiler_params=params(3),
    )(
        scalars,
        image_rows,
        held_rows,
        table,
        text[0],
        attn_gain[None],
        full_b,
        out_cols,
        cache_keys[0],
        cache_values[0],
        held_owner[0],
        owner_row,
        recompute_pos,
    )
    return result[None]


def solution(mesh):
    in_specs = (
        P("req", "mlp", None),
        P(),
        P("mlp", "req", None),
        P("req", None),
        P("req"),
        P("req"),
        P("req", None, None),
        P(),
        P(None, "req", "mlp"),
        P("mlp", "req"),
        P("req", None, "mlp"),
        P("req", None, "mlp"),
        P("req", None),
        P("req", None, None),
        P("req", None),
        P("req", None),
    )
    out_specs = P("req", None, "mlp")
    return jax.shard_map(local, mesh=mesh, in_specs=in_specs, out_specs=out_specs, check_vma=False)
```

time: 348 us -> 161 us (0.46)
  Pallas kernels: 0 us -> 136 us
  waiting for transfers between devices: 100 us -> 0 us
  blocking collectives: 63.4 us -> 0 us
  starting transfers between devices: 52 us -> 0 us
  local copies, waits for them, and re-layouts: 73.3 us -> 21.4 us
  matrix products: 23 us -> 0 us
  other arithmetic: 17.4 us -> 1.47 us
  between operations: 16.9 us -> 1.43 us
    pallas_call x0 -> x3, Pallas kernels: none -> 136 us  [the longest x1 72.5 us: local(): pl.pallas_call(gather_kernel, out_shape=(SD((2, NY, BLOCK, HALF), bf16),...]
    all_gather x2 -> x0, blocking collectives: 63.4 us -> none  [the longest x1 53.2 us: local(): lax.all_gather(out_weight, 'req', axis=1, tiled=True)]
    all_to_all x4 -> x0, starting transfers between devices: 51.9 us -> none  [the longest x1 18.4 us: local(): lax.all_to_all(image_counts.reshape(n_req, 1), 'req', split_axis=0, conca...]
    reduce_scatter x2 -> x0, waiting for transfers between devices: 41.7 us -> none  [the longest x1 31.5 us: local(): lax.psum_scatter(terms, 'mlp', scatter_dimension=1, tiled=True)]
    all_gather x2 -> x0, waiting for transfers between devices: 34.2 us -> none  [the longest x1 34.2 us: local(): weight_cols = lax.all_gather(qkv_weight, 'req', axis=1, tiled=True)]
    scatter x4 -> x0, local copies, waits for them, and re-layouts: 26.6 us -> none  [the longest x1 15.1 us: local(): outgoing = jnp.zeros((n_req, capacity, image_tokens.shape[1]), jnp.bfloat...]
    all_to_all x4 -> x0, waiting for transfers between devices: 23.3 us -> none  [the longest x1 16.7 us: local(): lax.all_to_all(picked, 'req', split_axis=0, concat_axis=0, tiled=True)]
    dot_general x9 -> x0, matrix products: 19.3 us -> none  [the longest x1 5.12 us: local(): jnp.dot(normed_patch, lax.all_gather(proj_weight, 'req', axis=1, tiled=Tr...]
  transfers between devices with their start and end apart: 8 -> 0, of which waited for: 5 -> 0; matrix products, arithmetic and copies ran while one was open for 20% -> 0% of each run, Pallas kernels for 0% -> 0%
where the time goes in v1:
time: 161 us; the launch traced here: 160 us
  Pallas kernels  136 us (84%)
  local copies, waits for them, and re-layouts  21.4 us (13%)
    pallas_call x1, Pallas kernels, local(): pl.pallas_call(gather_kernel, out_shape=(SD((2, NY, BLOCK, HALF), bf16),...  72.5 us
    pallas_call x1, Pallas kernels, local(): pl.pallas_call(image_kernel, out_shape=SD((NX, GROUP, 16, WINDOW), bf16),...  40.2 us
    pallas_call x1, Pallas kernels, local(): pl.pallas_call(attend_kernel, out_shape=SD((ROWS, LOCAL), bf16), in_specs...  22.9 us
    unnamed x42, local copies, waits for them, and re-layouts  16.5 us

profile of v1, /device:TPU:1, one launch (start us, length us, event | category | flops | bytes accessed | tf_op | source)
XLA Modules:
  0.0 159.9 jit_solution(3885485350926794926)
XLA Ops:
  0.0 0.9 fusion
  0.9 0.8 concatenate.10.wb_ref
  1.8 0.1 pad.2.clone
  1.8 0.7 multiply_add_fusion
  2.5 0.7 add_add_fusion.idx_ref
  3.2 1.0 copy-done.9
  4.2 0.0 copy-start.13
  4.2 0.9 copy-done.13
  5.1 0.0 copy-start.14
  5.1 0.8 copy-done.14
  5.9 72.5 %shard_map.163 = (bf16[2,8,160,640]{3,2,1,0:T(8,128)(2,1)S(1)}, bf16[2,8,160,640]{3,2,1,0:T(8,128)(2,1)}, bf16[4,2,160,384]{3,2,1,0:T(8,128)(2,1)S(1)}, bf16[4,8...) custom-call(bf16[10,1280]{1,0:T(8,128)(2,1)S(1)} %bitcast.23, bf16[10,1280]{1,0:T(8,128)(2,1)S(1)} %concatenate.10.wb_ref, ...), custom_call_target="tpu_custom_call" | custom-call | tf_op jit(solution)/shard_map/pallas_call | solution.py:595
  78.4 0.0 copy-start.2
  78.4 0.9 copy-done.2
  79.3 0.0 copy-start.4
  79.3 0.9 copy-done.4
  80.2 0.0 copy-start.11
  80.2 0.7 copy-done.11
  80.9 0.8 copy.21.dest_col
  81.6 0.7 broadcast_in_dim.12.gain_ref
  82.3 0.0 copy-start.8
  82.3 1.0 copy-done.8
  83.3 0.0 copy-start.15
  83.3 0.7 copy-done.15
  84.0 0.0 copy-start.16
  84.0 0.0 copy-start.18
  84.0 0.0 copy-start.17
  84.0 40.2 %shard_map.164.image_ref = bf16[4,16,16,384]{3,2,1,0:T(8,128)(2,1)S(1)} custom-call(bf16[128,1280]{1,0:T(8,128)(2,1)S(1)} %bitcast.22, f32[1,1280]{1,0:T(1,128)S(1)} %broadcast_in_dim.12.gain_ref, bf16[2,8,160,640]{3,2,1,0:T(8,128)(2,1)S(1)} %get-tuple-element.10.weight_ref, s32[128,1]{1,0:T(8,128)S(1)} %copy.21.dest_col, s32[1,128]{1,0:T(1,128)S(1)} %bitcast.25), custom_call_target="tpu_custom_call" | custom-call | tf_op jit(solution)/shard_map/pallas_call | solution.py:641
  124.2 0.0 copy-start
  124.2 0.9 copy-done
  125.1 0.0 copy-start.5
  125.1 1.7 %copy.23 = bf16[1,1280,320]{2,1,0:T(8,128)(2,1)S(1)} copy(bf16[1,1280,320]{1,2,0:T(8,128)(2,1)} %param.28) | data formatting | bytes 1638400 | tf_op args[11]
  126.8 1.7 %copy.22 = bf16[1,1280,320]{2,1,0:T(8,128)(2,1)S(1)} copy(bf16[1,1280,320]{1,2,0:T(8,128)(2,1)} %param.27) | data formatting | bytes 1638400 | tf_op args[10]
  128.5 0.0 copy-done.16
  128.5 0.7 copy.24.owner_col
  129.2 0.0 copy-done.18
  130.5 0.1 pad_add_fusion.scalars
  130.6 0.0 copy-done.17
  130.6 0.0 copy-done.5
  130.6 0.0 copy-done.1
  130.6 0.0 copy-start.3
  130.6 1.2 copy-done.3
  131.8 1.1 copy-done.7
  132.9 0.8 copy-done.10
  133.7 0.9 copy-done.12
  134.7 22.9 %shard_map.165 = bf16[256,320]{1,0:T(8,128)(2,1)S(1)} custom-call(s32[2]{0:T(128)S(1)} %pad_add_fusion.scalars, bf16[4,16,16,384]{3,2,1,0:T(8,128)(2,1)S(1)} %copy-done.1, bf16[4,8,32,384]{3,2,1,0:T(8,128)(2,1)S(1)} %copy-done.5, s32[16,2,8,128]{3,2,1,0:T(8,128)S(1)} %copy-done.12, bf16[256,1280]{1,0:T(8,128)(2,1)S(1)} %bitcast.21, ...), custom_call_target="tpu_custom_call" | custom-call | tf_op jit(solution)/shard_map/pallas_call | solution.py:665
  157.5 0.0 copy-start.6
  157.6 0.7 copy-done.6
  158.2 1.7 %copy.25 = bf16[1,256,320]{1,2,0:T(8,128)(2,1)} copy(bf16[1,256,320]{2,1,0:T(8,128)(2,1)} %bitcast.20) | data formatting | bytes 327680 | tf_op jit(solution)/shard_map/broadcast_in_dim | solution.py:695
  (9 shorter events, 0.0 us)
Async XLA Ops:
  3.2 1.0 copy-start.9
  4.2 0.9 copy-start.13
  5.1 0.8 copy-start.14
  78.4 0.9 copy-start.2
  79.3 0.9 copy-start.4
  80.2 0.7 copy-start.11
  82.3 1.0 copy-start.8
  83.3 0.7 copy-start.15
  84.0 44.5 %copy-start.16 = (s32[1,128,1]{1,2,0:T(1,128)S(1)}, s32[1,128,1]{1,2,0:T(1,128)}, u32[]{:S(2)}) copy-start(s32[1,128,1]{1,2,0:T(1,128)} %param.30) | copy-start | bytes 1540
  84.0 45.3 %copy-start.18 = (f32[1280]{0:T(1024)S(1)}, f32[1280]{0:T(1024)}, u32[]{:S(2)}) copy-start(f32[1280]{0:T(1024)} %param.24) | copy-start | bytes 15364
  84.0 46.6 %copy-start.17 = (s32[1,128]{1,0:T(1,128)S(1)}, s32[1,128]{1,0:T(1,128)}, u32[]{:S(2)}) copy-start(s32[1,128]{1,0:T(1,128)} %place_row.1) | copy-start | bytes 1540
  124.2 0.9 copy-start
  125.1 5.5 %copy-start.5 = (bf16[4,8,32,384]{3,2,1,0:T(8,128)(2,1)S(1)}, bf16[4,8,32,384]{3,2,1,0:T(8,128)(2,1)}, u32[]{:S(2)}) copy-start(bf16[4,8,32,384]{3,2,1,0:T(8,128)(2,1)} %copy-done.4) | copy-start | bytes 2359300
  125.1 5.5 %copy-start.1 = (bf16[4,16,16,384]{3,2,1,0:T(8,128)(2,1)S(1)}, bf16[4,16,16,384]{3,2,1,0:T(8,128)(2,1)}, u32[]{:S(2)}) copy-start(bf16[4,16,16,384]{3,2,1,0:T(8,128)(2,1)} %copy-done) | copy-start | bytes 2359300
  130.6 1.2 copy-start.3
  131.8 1.1 copy-start.7
  132.9 0.8 copy-start.10
  133.7 0.9 copy-start.12
  157.5 0.7 copy-start.6

commit v2 on v0

v2 whole, which is shorter than its diff:
```python
import functools

import jax
import jax.numpy as jnp
import numpy as np
from jax import lax
from jax.experimental import pallas as pl
from jax.experimental.pallas import tpu as pltpu
from jax.sharding import PartitionSpec as P

HEAD_DIM = 80
eps = 1e-06
big_negative = -1e30
MESH = pl.DeviceIdType.MESH
NZ, NY, NC, NX = 8, 8, 2, 4
GROUP = NY * NC
WIDTH = 1280
HALF = WIDTH // 2
SHARD = 10
PIECE = 16
BLOCK = GROUP * SHARD
WINDOW = 384
OFFSETS = (0, 256, 640, 896)
WIDTHS = (256, 384, 256, 384)
ROWS = 256
HEADS = 4
LOCAL = HEADS * HEAD_DIM
f32, bf16 = jnp.float32, jnp.bfloat16


def coords():
    r, m = lax.axis_index("req"), lax.axis_index("mlp")
    return r, m, lax.div(r, GROUP), lax.rem(lax.div(r, NC), NY), lax.rem(r, NC)


def at(z, y, c, m):
    return (z * GROUP + y * NC + c, m)


def send(src, dst, send_sem, recv_sem, device):
    copy = pltpu.make_async_remote_copy(
        src_ref=src,
        dst_ref=dst,
        send_sem=send_sem,
        recv_sem=recv_sem,
        device_id=device,
        device_id_type=MESH,
    )
    copy.start()
    return copy


def arrival(dst, send_sem, recv_sem, device):
    pltpu.make_async_remote_copy(
        src_ref=dst,
        dst_ref=dst,
        send_sem=send_sem,
        recv_sem=recv_sem,
        device_id=device,
        device_id_type=MESH,
    ).wait_recv()


def meet(devices):
    barrier = pltpu.get_barrier_semaphore()
    for device in devices:
        pl.semaphore_signal(barrier, inc=1, device_id=device, device_id_type=MESH)
    pl.semaphore_wait(barrier, len(devices))


def iota(shape, dim):
    return lax.broadcasted_iota(jnp.int32, shape, dim)


def hot(mask):
    return jnp.where(mask, 1.0, 0.0).astype(bf16)


def mm(a, b):
    return jnp.dot(a, b, preferred_element_type=f32)


def mm_t(a, b):
    return lax.dot_general(a, b, (((1,), (1,)), ((), ())), preferred_element_type=f32)


def norm(x, gain):
    scale = lax.rsqrt(jnp.mean(x * x, -1, keepdims=True) + eps)
    return (x * scale * gain).astype(bf16)


def swap_order(rows_first):
    a, b = iota((ROWS, ROWS), 0), iota((ROWS, ROWS), 1)
    if not rows_first:
        a, b = b, a
    other = (a & 7) * 32 + ((a >> 3) & 1) * 16 + (a >> 4)
    return hot(other == b)


class Ring:
    CHUNKS = 5
    ROWS = BLOCK // CHUNKS

    def __init__(self, full, own, c, place, near, sibling, sems):
        self.full, self.own, self.c, self.place = full, own, c, place
        self.near, self.sibling = near, sibling
        self.ssem, self.rsem = sems
        self.sent = []

    def block(self, half, number):
        return self.full.at[half, lax.rem(number + 2 * NZ, NZ)]

    def chunk(self, ref, k):
        return ref.at[pl.ds(k * self.ROWS, self.ROWS)]

    def push(self, src, dst, slot, device):
        self.sent.append(send(src, dst, self.ssem.at[slot], self.rsem.at[slot], device))

    def start(self, value):
        self.full[self.c, self.place] = value
        own = self.block(self.c, self.place)
        for k in range(self.CHUNKS):
            for side in range(2):
                part = self.chunk(own, k)
                self.push(part, part, side * 20 + k, self.near[side])
        self.push(own, own, 40, self.sibling)

    def step(self, s):
        sides = (-1, 1)
        for k in range(self.CHUNKS):
            for side in range(2):
                if s == 3 and (k < 3) != (side == 0):
                    continue
                slot = side * 20 + s * 5 + k
                part = self.chunk(self.block(self.c, self.place + sides[side] * (1 + s)), k)
                arrival(part, self.ssem.at[slot], self.rsem.at[slot], self.near[side])
                if s < 2 or (s == 2 and (k < 3) == (side == 0)):
                    self.push(part, part, slot + 5, self.near[side])
        for side in range(2):
            if s < 3 or side == 0:
                got = self.block(self.c, self.place + sides[side] * (1 + s))
                self.push(got, got, 41 + 2 * s + side, self.sibling)

    def finish(self, place):
        for slot, shift in ((40, 0), (41, -1), (42, 1), (43, -2), (44, 2), (45, -3), (46, 3), (47, -4)):
            got = self.block(1 - self.c, place + shift)
            arrival(got, self.ssem.at[slot], self.rsem.at[slot], self.sibling)


def to_col(row):
    eye = iota((128, 128), 0) == iota((128, 128), 1)
    return jnp.sum(jnp.where(eye, row.astype(f32), 0.0), -1, keepdims=True)


class Pairs:
    def __init__(self, c, sibling, turn, back, device, ssem, rsem, cores=NC):
        self.c, self.sibling, self.turn, self.back = c, sibling, turn, back
        self.device, self.ssem, self.rsem, self.cores = device, ssem, rsem, cores
        self.sent = []

    def spans(self):
        for d in range(1, 8):
            for k in range(self.cores):
                yield d, k, (self.c if k == 0 else 1 - self.c)

    def send(self, pick, dst, own):
        for d, k, h in self.spans():
            to = self.turn[d]
            self.sent.append(
                send(pick(to, h), dst, self.ssem.at[d, k], self.rsem.at[d, k], self.device(to, h))
            )
        if self.cores == 2:
            src = pick(own, 1 - self.c)
            self.sent.append(send(src, dst, self.ssem.at[0, 0], self.rsem.at[0, 0], self.sibling))

    def wait(self, spot, own):
        for d, k, h in self.spans():
            to = self.back[d]
            arrival(spot(to, h), self.ssem.at[d, k], self.rsem.at[d, k], self.device(to, h))
        if self.cores == 2:
            arrival(spot(own, 1 - self.c), self.ssem.at[0, 0], self.rsem.at[0, 0], self.sibling)


def kernel(
    image_pos,
    text_len,
    vis_gain,
    attn_gain,
    wa_hbm,
    wb_hbm,
    dest_hbm,
    owner_hbm,
    row_hbm,
    place_hbm,
    dense_hbm,
    patch_hbm,
    held_hbm,
    text_hbm,
    keys_hbm,
    values_hbm,
    result,
    wa,
    wb,
    small,
    dense,
    patch,
    held,
    text,
    keys,
    values,
    piece,
    stage_a,
    stage_b,
    full_a,
    full_b,
    idx,
    idx_stage,
    idx_own,
    table,
    order,
    normed,
    turned_cols,
    part,
    parts,
    picked_i,
    hop_i,
    turned_i,
    image,
    picked_h,
    hop_h,
    turned_h,
    held_in,
    out_cols,
    rows,
    mixed_all,
    local,
    sem_as,
    sem_ar,
    sem_bs,
    sem_br,
    sem_is,
    sem_ir,
    sem_ts,
    sem_tr,
    sem_hs,
    sem_hr,
    sem_gs,
    sem_gr,
    sem_zs,
    sem_zr,
    sem_ys,
    sem_yr,
    sem_xs,
    sem_xr,
    sem_ras,
    sem_rar,
    sem_rbs,
    sem_rbr,
):
    r, m, z, y, c = coords()
    yc = y * NC + c
    sibling = at(z, y, 1 - c, m)
    planes = [(r, lax.rem(m + d, NX)) for d in range(NX)]
    back_m = [lax.rem(m + NX - d, NX) for d in range(NX)]
    turn_y = [lax.rem(y + d, NY) for d in range(NY)]
    turn_z = [lax.rem(z + d, NZ) for d in range(NZ)]
    back_y = [lax.rem(y + NY - d, NY) for d in range(NY)]
    back_z = [lax.rem(z + NZ - d, NZ) for d in range(NZ)]

    loads = {}
    for number, (name, src, dst) in enumerate(
        (
            ("wa", wa_hbm, wa),
            ("wb", wb_hbm, wb),
            ("dest", dest_hbm, small.at[0]),
            ("owner", owner_hbm, small.at[1]),
            ("row", row_hbm, small.at[2]),
            ("place", place_hbm, small.at[3]),
            ("patch", patch_hbm, patch),
            ("dense", dense_hbm, dense),
            ("held", held_hbm, held),
            ("text", text_hbm, text),
            ("keys", keys_hbm, keys.at[:, pl.ds(0, WIDTH)]),
            ("values", values_hbm, values.at[:, pl.ds(0, WIDTH)]),
        )
    ):
        loads[name] = pltpu.make_async_copy(src, dst, local.at[number])
        loads[name].start()

    peers = [sibling] + planes[1:]
    peers += [at(z, turn_y[d], h, m) for d in range(1, NY) for h in range(NC)]
    peers += [at(turn_z[d], y, h, m) for d in range(1, NZ) for h in range(NC)]
    barrier = pltpu.get_barrier_semaphore()
    for device in peers:
        pl.semaphore_signal(barrier, inc=1, device_id=device, device_id_type=MESH)

    def same_z(p, h):
        return at(z, p, h, m)

    def same_y(p, h):
        return at(p, y, h, m)

    for name in ("wa", "wb", "dest", "owner", "row", "place"):
        loads[name].wait()
    for n, ref in ((0, wa), (1, wb)):
        for h in range(NC):
            piece[n, h] = jnp.zeros((PIECE, HALF), bf16)
            piece[n, h, 0:SHARD, :] = ref[:, h * HALF : (h + 1) * HALF]
    dest_row, owner_row = small[0], small[1]
    idx[...] = jnp.concatenate([dest_row, owner_row * 128 + small[2], jnp.zeros((6, 128), jnp.int32)], 0)
    pl.semaphore_wait(barrier, len(peers))
    sent = []

    mine = pl.ds(pl.multiple_of(z * 8, 8), 8)
    idx_stage[mine, :] = idx[...]
    for d in range(1, NZ):
        sent.append(send(idx, idx_stage.at[mine], sem_is.at[d], sem_ir.at[d], same_y(turn_z[d], c)))

    group = (1 - c) * z + c * y
    back_g = [lax.rem(group + 8 - d, 8) for d in range(8)]

    def spread(n, stage, ssem, rsem):
        kept = jnp.where(c == 0, piece[n, 0].astype(f32), piece[n, 1].astype(f32))
        stage[group * NC + c] = kept.astype(bf16)
        there = (1 - c) * y + c * z
        spot = stage.at[there * NC + c]
        sent.append(send(piece.at[n, 1 - c], spot, ssem.at[0, 0], rsem.at[0, 0], sibling))
        for d in range(1, 8):
            spot = stage.at[z * NC + c]
            sent.append(send(piece.at[n, 0], spot, ssem.at[d, 0], rsem.at[d, c], same_y(turn_z[d], 0)))
            spot = stage.at[y * NC + c]
            sent.append(send(piece.at[n, 1], spot, ssem.at[d, 1], rsem.at[d, c], same_z(turn_y[d], 1)))

    def gathered(stage, ssem, rsem):
        arrival(stage.at[group * NC + 1 - c], ssem.at[0, 0], rsem.at[0, 0], sibling)
        for d in range(1, 8):
            for k in range(NC):
                spot = stage.at[back_g[d] * NC + k]
                arrival(spot, ssem.at[d, 0], rsem.at[d, k], sibling)
        return mm(dense[...], stage[...].reshape(GROUP * PIECE, HALF)).astype(bf16)

    spread(0, stage_a, sem_as, sem_ar)

    loads["patch"].wait()
    xn = norm(patch[...].astype(f32), vis_gain[...].reshape(1, WIDTH))
    j = iota((1, WIDTH), 1)
    source = lax.div(lax.rem(j, 160), 20) * 160 + lax.div(j, 160) * 20 + lax.rem(j, 20)
    for b in range(5):
        span = slice(b * 256, (b + 1) * 256)
        order[span, :] = hot(iota((256, WIDTH), 0) + b * 256 == source)
    normed[0:128, :] = xn
    turned_cols[0:128, :] = mm(xn, order[...]).astype(bf16)

    for d in range(1, NZ):
        got = idx_stage.at[pl.ds(pl.multiple_of(back_z[d] * 8, 8), 8)]
        arrival(got, sem_is.at[d], sem_ir.at[d], same_y(back_z[d], c))
    for which in range(2):
        idx_own[which] = idx_stage[pl.ds(which, NZ, stride=8), :]
    table[yc] = idx_own[...]
    tables = Pairs(c, sibling, turn_y, back_y, same_z, sem_ts, sem_tr)
    tables.send(lambda p, h: idx_own, table.at[yc], y)

    place = (1 - c) * y + c * z
    there = (1 - c) * z + c * y

    def ring_device(p):
        return ((1 - c) * (z * GROUP + p * NC) + c * (p * GROUP + y * NC + 1), m)

    near = [ring_device(lax.rem(place + 1, 8)), ring_device(lax.rem(place + 7, 8))]
    ring_a = Ring(full_a, None, c, place, near, sibling, (sem_ras, sem_rar))
    ring_b = Ring(full_b, None, c, place, near, sibling, (sem_rbs, sem_rbr))
    loads["dense"].wait()
    ring_a.start(gathered(stage_a, sem_as, sem_ar))
    spread(1, stage_b, sem_bs, sem_br)
    ring_a.step(0)

    tables.wait(lambda p, h: table.at[p * NC + h], y)
    code = table[:, 1]
    asked = (code >> 7) == r
    row = (code & 127).astype(f32)
    lane = iota((GROUP, NZ, 128), 2).astype(f32)
    first = jnp.min(jnp.where(asked, lane, 1000.0), -1, keepdims=True)
    want0 = jnp.sum(jnp.where(asked & (lane == first), row, 0.0), -1, keepdims=True)
    want1 = jnp.sum(jnp.where(asked, row, 0.0), -1, keepdims=True) - want0
    pick0 = jnp.where(lane == want0, 1.0, 0.0)
    pick1 = jnp.where(lane == want1, 1.0, 0.0)
    pick = jnp.concatenate([pick0, pick1], 1).reshape(ROWS, 128).astype(bf16)
    base = pl.multiple_of(m * 320 - lax.rem(m, 2) * 64, 128)
    loads["held"].wait()
    picked_h[...] = mm(pick, held[:, pl.ds(base, WINDOW)]).astype(bf16).reshape(GROUP, 16, WINDOW)
    ring_a.step(1)
    hop_h[yc] = picked_h[yc]
    held_y = Pairs(c, sibling, turn_y, back_y, same_z, sem_hs, sem_hr)
    held_y.send(lambda p, h: picked_h.at[p * NC + h], hop_h.at[yc], y)

    own_b = gathered(stage_b, sem_bs, sem_br)
    ring_a.step(2)
    ring_b.start(own_b)
    ring_a.step(3)

    held_y.wait(lambda p, h: hop_h.at[p * NC + h], y)
    back = mm(swap_order(False), hop_h[...].reshape(ROWS, WINDOW)).astype(bf16)
    turned_h[...] = back.reshape(NZ, 32, WINDOW)
    held_in[m, z] = turned_h[z]
    held_z = Pairs(c, sibling, turn_z, back_z, same_y, sem_gs, sem_gr, 1)
    held_z.send(lambda p, h: turned_h.at[p], held_in.at[m, z], z)

    ring_a.finish(there)
    left = mm(turned_cols[0:128, :], full_a[0].reshape(WIDTH, HALF))
    part[0] = left[:, 0:384]
    part[1] = left[:, 256:640]
    right = mm(normed[0:128, :], full_a[1].reshape(WIDTH, HALF))
    part[2] = right[:, 0:384]
    part[3] = right[:, 256:640]
    for d in range(1, NX):
        sent.append(send(part.at[planes[d][1]], parts.at[m], sem_xs.at[0, d], sem_xr.at[0, d], planes[d]))
    ring_b.step(0)

    dest_col = to_col(dest_row)
    earlier = (dest_col == dest_row.astype(f32)) & (iota((128, 128), 0) < iota((128, 128), 1))
    rank = jnp.sum(jnp.where(earlier, 1.0, 0.0), 0, keepdims=True)
    q = iota((ROWS, 128), 0)
    target = (q >> 5) * 16 + (q & 15)
    slot = ((q >> 4) & 1).astype(f32)
    choose = hot((dest_row == target) & (rank == slot))
    turn = swap_order(True)

    held_z.wait(lambda p, h: held_in.at[m, p], z)
    ring_b.step(1)
    total = part[m]
    for d in range(1, NX):
        arrival(parts.at[back_m[d]], sem_xs.at[0, d], sem_xr.at[0, d], (r, back_m[d]))
        total = total + parts[back_m[d]]
    picked_i[...] = mm(choose, total.astype(bf16)).astype(bf16).reshape(NZ, 32, WINDOW)
    hop_i[z] = picked_i[z]
    image_z = Pairs(c, sibling, turn_z, back_z, same_y, sem_zs, sem_zr, 1)
    image_z.send(lambda p, h: picked_i.at[p], hop_i.at[z], z)
    for d in range(1, NX):
        sent.append(send(held_in.at[m], held_in.at[m], sem_xs.at[1, d], sem_xr.at[1, d], planes[d]))
    ring_b.step(2)
    image_z.wait(lambda p, h: hop_i.at[p], z)
    turned_i[...] = mm(turn, hop_i[...].reshape(ROWS, WINDOW)).astype(bf16).reshape(GROUP, 16, WINDOW)
    image[m, yc] = turned_i[yc]
    image_y = Pairs(c, sibling, turn_y, back_y, same_z, sem_ys, sem_yr)
    image_y.send(lambda p, h: turned_i.at[p * NC + h], image.at[m, yc], y)
    ring_b.step(3)
    ring_b.finish(there)
    image_y.wait(lambda p, h: image.at[m, p * NC + h], y)
    for d in range(1, NX):
        sent.append(send(image.at[m], image.at[m], sem_xs.at[2, d], sem_xr.at[2, d], planes[d]))

    def columns(plane):
        return full_b.at[1, pl.ds(plane * 2, 2), :, pl.ds(0, WINDOW)]

    for d in range(1, NX):
        src = columns(planes[d][1])
        sent.append(send(src, out_cols.at[m], sem_xs.at[3, d], sem_xr.at[3, d], planes[d]))
    out_cols[m] = full_b[1, pl.ds(m * 2, 2), :, 0:WINDOW]

    gain = attn_gain[...].reshape(1, WIDTH)
    owner_col = to_col(owner_row)
    same = (owner_col == owner_row.astype(f32)) & (iota((128, 128), 1) < iota((128, 128), 0))
    rank = jnp.sum(jnp.where(same, 1.0, 0.0), -1, keepdims=True).astype(jnp.int32)
    owner = owner_col.astype(jnp.int32)
    spot = (owner >> 4) * 32 + rank * 16 + (owner & 15)
    fetch = hot(spot == iota((128, ROWS), 1))
    for d in range(1, NX):
        arrival(held_in.at[back_m[d]], sem_xs.at[1, d], sem_xr.at[1, d], (r, back_m[d]))
    for b in range(NX):
        o, w = OFFSETS[b], WIDTHS[b]
        rows[0:128, o : o + w] = mm(fetch, held_in[b].reshape(ROWS, WINDOW)[:, 0:w])
    eye = hot(iota((LOCAL, LOCAL), 0) == iota((LOCAL, LOCAL), 1))

    def keys_and_values(count):
        xk = mm(turned_cols[0:count, :], full_b[0].reshape(WIDTH, HALF)[:, 256:640])
        xv = mm(normed[0:count, :], full_b[1].reshape(WIDTH, HALF)[:, 256:640])
        return (
            mm_t(eye, xk.astype(bf16)[:, 64:384]).astype(bf16),
            mm_t(eye, xv.astype(bf16)[:, 64:384]).astype(bf16),
        )

    xn = norm(rows[0:128, :], gain)
    normed[0:128, :] = xn
    turned_cols[0:128, :] = mm(xn, order[...]).astype(bf16)
    fresh = keys_and_values(128)
    loads["keys"].wait()
    loads["values"].wait()
    place_col = to_col(small[3]).astype(jnp.int32)
    for b in range(5):
        span = slice(b * 256, (b + 1) * 256)
        match = place_col == iota((128, 256), 1) + b * 256
        put = hot(match)
        hit = jnp.sum(jnp.where(match, 1.0, 0.0), 0, keepdims=True) > 0.0
        for cached, new in ((keys, fresh[0]), (values, fresh[1])):
            cached[:, span] = jnp.where(hit, mm(new, put), cached[:, span].astype(f32)).astype(bf16)

    named = hot(table[:, 0].reshape(128, 128) == r)
    counts = mm_t(jnp.ones((8, 128), bf16), named)
    s0, s1 = iota((128, 128), 0), iota((128, 128), 1)
    ahead = hot((s0 & 7) * 16 + (s0 >> 3) < (s1 & 7) * 16 + (s1 >> 3))
    before = mm(counts.astype(bf16), ahead)
    s, a = iota((128, ROWS), 0), iota((128, ROWS), 1)
    widen = hot(((s >> 3) == (a >> 4)) & ((s & 7) == (a & 7)))
    counts_a = mm(counts.astype(bf16), widen)[0:1]
    before_a = mm(before.astype(bf16), widen)[0:1]
    slot = ((iota((1, ROWS), 1) >> 3) & 1).astype(f32)
    number = jnp.sum(counts[0:1], -1, keepdims=True)
    wanted = jnp.full((1, 1), image_pos[0], jnp.int32).astype(f32)
    start = jnp.minimum(wanted, ROWS - number)
    length = jnp.minimum(float(ROWS), jnp.full((1, 1), text_len[0], jnp.int32).astype(f32) + number)
    q = iota((ROWS, ROWS), 0).astype(f32)
    t = iota((ROWS, ROWS), 1).astype(f32)
    choose = hot((before_a + slot == q - start) & (counts_a > slot))
    take = hot(((q < start) & (t == q)) | ((q >= start + number) & (t == q - number)))
    loads["text"].wait()
    for b in range(NX):
        o, w = OFFSETS[b], WIDTHS[b]
        rows[:, o : o + w] = mm(take, text[:, o : o + w])
    for d in range(1, NX):
        arrival(image.at[back_m[d]], sem_xs.at[2, d], sem_xr.at[2, d], (r, back_m[d]))
    for b in range(NX):
        o, w = OFFSETS[b], WIDTHS[b]
        rows[:, o : o + w] += mm(choose, image[b].reshape(ROWS, WINDOW)[:, 0:w])

    xn = norm(rows[...], gain)
    normed[...] = xn
    turned_cols[...] = mm(xn, order[...]).astype(bf16)
    queries = mm(turned_cols[...], full_b[0].reshape(WIDTH, HALF)[:, 0:384]).astype(bf16)
    new_keys, new_values = keys_and_values(ROWS)
    keys[:, WIDTH:] = new_keys
    values[:, WIDTH:] = new_values

    factor = HEAD_DIM ** (-0.5) * float(np.log2(np.e))
    for i in range(2):
        span = slice(i * 128, (i + 1) * 128)
        count = 128 * (i + 1)
        qi = iota((128, count), 0) + i * 128
        ti = iota((128, count), 1)
        seen = (ti <= qi) & (ti.astype(f32) < length)
        live = (iota((HEAD_DIM, 128), 1) + i * 128).astype(f32) < length
        for h in range(HEADS):
            lanes = slice(h * HEAD_DIM, (h + 1) * HEAD_DIM)
            head = queries[span, lanes]
            old = mm(head, keys[lanes, 0:WIDTH])
            new = jnp.where(seen, mm(head, keys[lanes, WIDTH : WIDTH + count]), big_negative)
            highest = jnp.maximum(jnp.max(old, -1, keepdims=True), jnp.max(new, -1, keepdims=True))
            old = jnp.exp2((old - highest) * factor)
            new = jnp.exp2((new - highest) * factor)
            inverse = 1.0 / (jnp.sum(old, -1, keepdims=True) + jnp.sum(new, -1, keepdims=True))
            old, new = (old * inverse).astype(bf16), (new * inverse).astype(bf16)
            summed = mm_t(values[lanes, 0:WIDTH], old) + mm_t(values[lanes, WIDTH : WIDTH + count], new)
            mixed_all[m, i, lanes, :] = jnp.where(live, summed, 0.0).astype(bf16)
        for d in range(1, NX):
            half = mixed_all.at[m, i]
            sent.append(send(half, half, sem_xs.at[4 + i, d], sem_xr.at[4 + i, d], planes[d]))

    def product(plane, i):
        return mm(out_cols[plane].reshape(LOCAL, WINDOW)[:, 0:LOCAL], mixed_all[plane, i])

    for d in range(1, NX):
        arrival(out_cols.at[back_m[d]], sem_xs.at[3, d], sem_xr.at[3, d], (r, back_m[d]))
    for i in range(2):
        terms = product(m, i)
        for d in range(1, NX):
            arrival(mixed_all.at[back_m[d], i], sem_xs.at[4 + i, d], sem_xr.at[4 + i, d], (r, back_m[d]))
            terms = terms + product(back_m[d], i)
        result[:, i * 128 : (i + 1) * 128] = terms.astype(bf16)
    for group_sent in (tables, held_y, held_z, image_z, image_y, ring_a, ring_b):
        sent += group_sent.sent
    for copy in sent:
        copy.wait_send()


VM = functools.partial(pl.BlockSpec, memory_space=pltpu.VMEM)
HB = functools.partial(pl.BlockSpec, memory_space=pl.ANY)
SM = functools.partial(pl.BlockSpec, memory_space=pltpu.SMEM)
SD = jax.ShapeDtypeStruct
DMA = pltpu.SemaphoreType.DMA


def local(
    patches,
    vis_gain,
    proj_weight,
    image_dest,
    image_pos,
    text_len,
    text,
    attn_gain,
    qkv_weight,
    out_weight,
    cache_keys,
    cache_values,
    held,
    held_owner,
    held_row,
    recompute_pos,
):
    wb = jnp.concatenate([qkv_weight[0], qkv_weight[1], out_weight.T, qkv_weight[2]], 1)
    k, p = np.arange(BLOCK)[:, None], np.arange(GROUP * PIECE)[None, :]
    dense = jnp.asarray((p == k // SHARD * PIECE + k % SHARD).astype(np.float32)).astype(bf16)
    V = pltpu.VMEM
    result = pl.pallas_call(
        kernel,
        out_shape=SD((LOCAL, ROWS), bf16),
        in_specs=[SM(), SM(), VM(), VM()] + [HB()] * 12,
        out_specs=VM(),
        scratch_shapes=[
            V((SHARD, WIDTH), bf16),
            V((SHARD, WIDTH), bf16),
            V((4, 1, 128), jnp.int32),
            V((BLOCK, GROUP * PIECE), bf16),
            V((128, WIDTH), bf16),
            V((128, WIDTH), bf16),
            V((ROWS, WIDTH), bf16),
            V((LOCAL, WIDTH + ROWS), bf16),
            V((LOCAL, WIDTH + ROWS), bf16),
            V((2, 2, PIECE, HALF), bf16),
            V((GROUP, PIECE, HALF), bf16),
            V((GROUP, PIECE, HALF), bf16),
            V((2, 8, BLOCK, HALF), bf16),
            V((2, 8, BLOCK, HALF), bf16),
            V((8, 128), jnp.int32),
            V((64, 128), jnp.int32),
            V((2, NZ, 128), jnp.int32),
            V((GROUP, 2, NZ, 128), jnp.int32),
            V((WIDTH, WIDTH), bf16),
            V((ROWS, WIDTH), bf16),
            V((ROWS, WIDTH), bf16),
            V((NX, 128, WINDOW), f32),
            V((NX, 128, WINDOW), f32),
            V((NZ, 32, WINDOW), bf16),
            V((NZ, 32, WINDOW), bf16),
            V((GROUP, 16, WINDOW), bf16),
            V((NX, GROUP, 16, WINDOW), bf16),
            V((GROUP, 16, WINDOW), bf16),
            V((GROUP, 16, WINDOW), bf16),
            V((NZ, 32, WINDOW), bf16),
            V((NX, NZ, 32, WINDOW), bf16),
            V((NX, 2, BLOCK, WINDOW), bf16),
            V((ROWS, WIDTH), f32),
            V((NX, 2, LOCAL, 128), bf16),
            DMA((12,)),
            DMA((8, 2)),
            DMA((8, 2)),
            DMA((8, 2)),
            DMA((8, 2)),
            DMA((8,)),
            DMA((8,)),
            DMA((8, 2)),
            DMA((8, 2)),
            DMA((8, 2)),
            DMA((8, 2)),
            DMA((8, 2)),
            DMA((8, 2)),
            DMA((8, 2)),
            DMA((8, 2)),
            DMA((8, 2)),
            DMA((8, 2)),
            DMA((6, NX)),
            DMA((6, NX)),
            DMA((48,)),
            DMA((48,)),
            DMA((48,)),
            DMA((48,)),
        ],
        compiler_params=pltpu.CompilerParams(
            collective_id=1, has_side_effects=True, vmem_limit_bytes=56 * 1024 * 1024
        ),
    )(
        image_pos,
        text_len,
        vis_gain,
        attn_gain,
        proj_weight[0],
        wb,
        image_dest.reshape(1, 128),
        held_owner.reshape(1, 128),
        held_row,
        recompute_pos,
        dense,
        patches[:, 0],
        held,
        text[0],
        cache_keys[0].T,
        cache_values[0].T,
    )
    return result.T[None]


def solution(mesh):
    in_specs = (
        P("req", "mlp", None),
        P(),
        P("mlp", "req", None),
        P("req", None),
        P("req"),
        P("req"),
        P("req", None, None),
        P(),
        P(None, "req", "mlp"),
        P("mlp", "req"),
        P("req", None, "mlp"),
        P("req", None, "mlp"),
        P("req", None),
        P("req", None, None),
        P("req", None),
        P("req", None),
    )
    out_specs = P("req", None, "mlp")
    return jax.shard_map(local, mesh=mesh, in_specs=in_specs, out_specs=out_specs, check_vma=False)
```

time: 348 us -> 109 us (0.31)
  Pallas kernels: 0 us -> 104 us
  waiting for transfers between devices: 100 us -> 0 us
  local copies, waits for them, and re-layouts: 73.3 us -> 3.92 us
  blocking collectives: 63.4 us -> 0 us
  starting transfers between devices: 52 us -> 0 us
  matrix products: 23 us -> 0 us
  other arithmetic: 17.4 us -> 0 us
  between operations: 16.9 us -> 1.33 us
    pallas_call x0 -> x1, Pallas kernels: none -> 104 us  [local(): pl.pallas_call(kernel, out_shape=SD((LOCAL, ROWS), bf16), in_specs=[SM(),...]
    all_gather x2 -> x0, blocking collectives: 63.4 us -> none  [the longest x1 53.2 us: local(): lax.all_gather(out_weight, 'req', axis=1, tiled=True)]
    all_to_all x4 -> x0, starting transfers between devices: 51.9 us -> none  [the longest x1 18.4 us: local(): lax.all_to_all(image_counts.reshape(n_req, 1), 'req', split_axis=0, conca...]
    reduce_scatter x2 -> x0, waiting for transfers between devices: 41.7 us -> none  [the longest x1 31.5 us: local(): lax.psum_scatter(terms, 'mlp', scatter_dimension=1, tiled=True)]
    all_gather x2 -> x0, waiting for transfers between devices: 34.2 us -> none  [the longest x1 34.2 us: local(): weight_cols = lax.all_gather(qkv_weight, 'req', axis=1, tiled=True)]
    scatter x4 -> x0, local copies, waits for them, and re-layouts: 26.6 us -> none  [the longest x1 15.1 us: local(): outgoing = jnp.zeros((n_req, capacity, image_tokens.shape[1]), jnp.bfloat...]
    all_to_all x4 -> x0, waiting for transfers between devices: 23.3 us -> none  [the longest x1 16.7 us: local(): lax.all_to_all(picked, 'req', split_axis=0, concat_axis=0, tiled=True)]
    dot_general x9 -> x0, matrix products: 19.3 us -> none  [the longest x1 5.12 us: local(): jnp.dot(normed_patch, lax.all_gather(proj_weight, 'req', axis=1, tiled=Tr...]
  transfers between devices with their start and end apart: 8 -> 0, of which waited for: 5 -> 0; matrix products, arithmetic and copies ran while one was open for 20% -> 0% of each run, Pallas kernels for 0% -> 0%
where the time goes in v2:
time: 109 us
  Pallas kernels  104 us (95%)
  local copies, waits for them, and re-layouts  3.92 us (4%)
  between operations  1.33 us (1%)
    pallas_call x1, Pallas kernels, local(): pl.pallas_call(kernel, out_shape=SD((LOCAL, ROWS), bf16), in_specs=[SM(),...  104 us
    unnamed x4, local copies, waits for them, and re-layouts  2.29 us

profile of v2, /device:TPU:1, one launch (start us, length us, event | category | flops | bytes accessed | tf_op | source)
XLA Modules:
  0.0 108.8 jit_solution(12972138490080093942)
XLA Ops:
  1.3 0.9 fusion
  2.2 0.0 copy-start
  2.3 0.7 copy-done
  2.9 0.7 concatenate.3.wb_hbm
  3.6 103.6 %shard_map.163 = bf16[320,256]{1,0:T(8,128)(2,1)} custom-call(s32[1]{0:T(128)S(6)} %copy.29.image_pos, s32[1]{0:T(128)S(6)} %copy.30.text_len, f32[1280]{0:T(1024)} %vis_gain.1, f32[1280]{0:T(1024)} %attn_gain.1, bf16[10,1280]{1,0:T(8,128)(2,1)} %bitcast.28, bf16[10,1280]{1,0:T(8,128)(2,1)} %concatenate.3.wb_hbm, s32[1,128]{1,0:T(1,128)} %bitcast.30, ...), custom_call_target="tpu_custom_call" | custom-call | tf_op jit(solution)/shard_map/pallas_call | solution.py:603
  107.2 1.6 %copy.31 = bf16[1,256,320]{1,2,0:T(8,128)(2,1)} copy(bf16[1,256,320]{1,2,0:T(8,128)(2,1)} %bitcast.25) | data formatting | bytes 327680
  (2 shorter events, 0.0 us)
Async XLA Ops:
  2.2 0.7 copy-start

commit v3 on v2

--- a/solution.py
+++ b/solution.py
@@ -20,6 +20,8 @@
 PIECE = 16
 BLOCK = GROUP * SHARD
 WINDOW = 384
+CHUNKS = 3
+FIRST = (0, 2, 5, 7)
 OFFSETS = (0, 256, 640, 896)
 WIDTHS = (256, 384, 256, 384)
 ROWS = 256
@@ -163,13 +165,15 @@
             for k in range(self.cores):
                 yield d, k, (self.c if k == 0 else 1 - self.c)
 
-    def send(self, pick, dst, own):
+    def send(self, pick, dst, own, distances=range(8)):
         for d, k, h in self.spans():
+            if d not in distances:
+                continue
             to = self.turn[d]
             self.sent.append(
                 send(pick(to, h), dst, self.ssem.at[d, k], self.rsem.at[d, k], self.device(to, h))
             )
-        if self.cores == 2:
+        if self.cores == 2 and 0 in distances:
             src = pick(own, 1 - self.c)
             self.sent.append(send(src, dst, self.ssem.at[0, 0], self.rsem.at[0, 0], self.sibling))
 
@@ -192,7 +196,6 @@
     owner_hbm,
     row_hbm,
     place_hbm,
-    dense_hbm,
     patch_hbm,
     held_hbm,
     text_hbm,
@@ -218,6 +221,7 @@
     idx_own,
     table,
     order,
+    ordered,
     normed,
     turned_cols,
     part,
@@ -229,10 +233,13 @@
     picked_h,
     hop_h,
     turned_h,
+    hop_back,
     held_in,
-    out_cols,
     rows,
-    mixed_all,
+    mixed,
+    product,
+    shares,
+    others,
     local,
     sem_as,
     sem_ar,
@@ -250,6 +257,10 @@
     sem_zr,
     sem_ys,
     sem_yr,
+    sem_ps,
+    sem_pr,
+    sem_qs,
+    sem_qr,
     sem_xs,
     sem_xr,
     sem_ras,
@@ -277,7 +288,6 @@
             ("row", row_hbm, small.at[2]),
             ("place", place_hbm, small.at[3]),
             ("patch", patch_hbm, patch),
-            ("dense", dense_hbm, dense),
             ("held", held_hbm, held),
             ("text", text_hbm, text),
             ("keys", keys_hbm, keys.at[:, pl.ds(0, WIDTH)]),
@@ -340,6 +350,7 @@
         return mm(dense[...], stage[...].reshape(GROUP * PIECE, HALF)).astype(bf16)
 
     spread(0, stage_a, sem_as, sem_ar)
+    spread(1, stage_b, sem_bs, sem_br)
 
     loads["patch"].wait()
     xn = norm(patch[...].astype(f32), vis_gain[...].reshape(1, WIDTH))
@@ -349,17 +360,15 @@
         span = slice(b * 256, (b + 1) * 256)
         order[span, :] = hot(iota((256, WIDTH), 0) + b * 256 == source)
     normed[0:128, :] = xn
-    turned_cols[0:128, :] = mm(xn, order[...]).astype(bf16)
+    turned_cols[...] = mm(xn, order[...]).astype(bf16)
+    k = iota((BLOCK, 1), 0)
+    dense[...] = hot(iota((BLOCK, GROUP * PIECE), 1) == lax.div(k, SHARD) * PIECE + lax.rem(k, SHARD))
 
     for d in range(1, NZ):
         got = idx_stage.at[pl.ds(pl.multiple_of(back_z[d] * 8, 8), 8)]
         arrival(got, sem_is.at[d], sem_ir.at[d], same_y(back_z[d], c))
     for which in range(2):
         idx_own[which] = idx_stage[pl.ds(which, NZ, stride=8), :]
-    table[yc] = idx_own[...]
-    tables = Pairs(c, sibling, turn_y, back_y, same_z, sem_ts, sem_tr)
-    tables.send(lambda p, h: idx_own, table.at[yc], y)
-
     place = (1 - c) * y + c * z
     there = (1 - c) * z + c * y
 
@@ -369,13 +378,16 @@
     near = [ring_device(lax.rem(place + 1, 8)), ring_device(lax.rem(place + 7, 8))]
     ring_a = Ring(full_a, None, c, place, near, sibling, (sem_ras, sem_rar))
     ring_b = Ring(full_b, None, c, place, near, sibling, (sem_rbs, sem_rbr))
-    loads["dense"].wait()
+    tables = []
+    for n in range(2):
+        table[n, yc] = idx_own[n]
+        tables.append(Pairs(c, sibling, turn_y, back_y, same_z, sem_ts.at[n], sem_tr.at[n]))
+    tables[1].send(lambda p, h: idx_own.at[1], table.at[1, yc], y)
     ring_a.start(gathered(stage_a, sem_as, sem_ar))
-    spread(1, stage_b, sem_bs, sem_br)
     ring_a.step(0)
 
-    tables.wait(lambda p, h: table.at[p * NC + h], y)
-    code = table[:, 1]
+    tables[1].wait(lambda p, h: table.at[1, p * NC + h], y)
+    code = table[1]
     asked = (code >> 7) == r
     row = (code & 127).astype(f32)
     lane = iota((GROUP, NZ, 128), 2).astype(f32)
@@ -388,33 +400,24 @@
     base = pl.multiple_of(m * 320 - lax.rem(m, 2) * 64, 128)
     loads["held"].wait()
     picked_h[...] = mm(pick, held[:, pl.ds(base, WINDOW)]).astype(bf16).reshape(GROUP, 16, WINDOW)
-    ring_a.step(1)
     hop_h[yc] = picked_h[yc]
     held_y = Pairs(c, sibling, turn_y, back_y, same_z, sem_hs, sem_hr)
-    held_y.send(lambda p, h: picked_h.at[p * NC + h], hop_h.at[yc], y)
-
-    own_b = gathered(stage_b, sem_bs, sem_br)
-    ring_a.step(2)
-    ring_b.start(own_b)
-    ring_a.step(3)
-
-    held_y.wait(lambda p, h: hop_h.at[p * NC + h], y)
-    back = mm(swap_order(False), hop_h[...].reshape(ROWS, WINDOW)).astype(bf16)
-    turned_h[...] = back.reshape(NZ, 32, WINDOW)
-    held_in[m, z] = turned_h[z]
-    held_z = Pairs(c, sibling, turn_z, back_z, same_y, sem_gs, sem_gr, 1)
-    held_z.send(lambda p, h: turned_h.at[p], held_in.at[m, z], z)
+    for step, distances in ((1, (0, 1, 2)), (2, (3, 4, 5)), (3, (6, 7))):
+        held_y.send(lambda p, h: picked_h.at[p * NC + h], hop_h.at[yc], y, distances)
+        ring_a.step(step)
+    ring_b.start(gathered(stage_b, sem_bs, sem_br))
 
     ring_a.finish(there)
-    left = mm(turned_cols[0:128, :], full_a[0].reshape(WIDTH, HALF))
-    part[0] = left[:, 0:384]
-    part[1] = left[:, 256:640]
+    left = mm(turned_cols[...], full_a[0].reshape(WIDTH, HALF))
+    for b in range(5):
+        part[b] = left[:, b * 128 : (b + 1) * 128]
     right = mm(normed[0:128, :], full_a[1].reshape(WIDTH, HALF))
-    part[2] = right[:, 0:384]
-    part[3] = right[:, 256:640]
-    for d in range(1, NX):
-        sent.append(send(part.at[planes[d][1]], parts.at[m], sem_xs.at[0, d], sem_xr.at[0, d], planes[d]))
-    ring_b.step(0)
+    for b in range(5):
+        part[5 + b] = right[:, b * 128 : (b + 1) * 128]
+    for k in range(CHUNKS):
+        for d in range(1, NX):
+            src = part.at[lax.div(planes[d][1] * 5, 2) + k]
+            sent.append(send(src, parts.at[m, k], sem_ps.at[k, d], sem_pr.at[k, d], planes[d]))
 
     dest_col = to_col(dest_row)
     earlier = (dest_col == dest_row.astype(f32)) & (iota((128, 128), 0) < iota((128, 128), 1))
@@ -424,64 +427,82 @@
     slot = ((q >> 4) & 1).astype(f32)
     choose = hot((dest_row == target) & (rank == slot))
     turn = swap_order(True)
-
-    held_z.wait(lambda p, h: held_in.at[m, p], z)
-    ring_b.step(1)
-    total = part[m]
-    for d in range(1, NX):
-        arrival(parts.at[back_m[d]], sem_xs.at[0, d], sem_xr.at[0, d], (r, back_m[d]))
-        total = total + parts[back_m[d]]
-    picked_i[...] = mm(choose, total.astype(bf16)).astype(bf16).reshape(NZ, 32, WINDOW)
-    hop_i[z] = picked_i[z]
-    image_z = Pairs(c, sibling, turn_z, back_z, same_y, sem_zs, sem_zr, 1)
-    image_z.send(lambda p, h: picked_i.at[p], hop_i.at[z], z)
-    for d in range(1, NX):
-        sent.append(send(held_in.at[m], held_in.at[m], sem_xs.at[1, d], sem_xr.at[1, d], planes[d]))
-    ring_b.step(2)
-    image_z.wait(lambda p, h: hop_i.at[p], z)
-    turned_i[...] = mm(turn, hop_i[...].reshape(ROWS, WINDOW)).astype(bf16).reshape(GROUP, 16, WINDOW)
-    image[m, yc] = turned_i[yc]
-    image_y = Pairs(c, sibling, turn_y, back_y, same_z, sem_ys, sem_yr)
-    image_y.send(lambda p, h: turned_i.at[p * NC + h], image.at[m, yc], y)
-    ring_b.step(3)
-    ring_b.finish(there)
-    image_y.wait(lambda p, h: image.at[m, p * NC + h], y)
-    for d in range(1, NX):
-        sent.append(send(image.at[m], image.at[m], sem_xs.at[2, d], sem_xr.at[2, d], planes[d]))
-
-    def columns(plane):
-        return full_b.at[1, pl.ds(plane * 2, 2), :, pl.ds(0, WINDOW)]
-
-    for d in range(1, NX):
-        src = columns(planes[d][1])
-        sent.append(send(src, out_cols.at[m], sem_xs.at[3, d], sem_xr.at[3, d], planes[d]))
-    out_cols[m] = full_b[1, pl.ds(m * 2, 2), :, 0:WINDOW]
-
-    gain = attn_gain[...].reshape(1, WIDTH)
+    image_z = [Pairs(c, sibling, turn_z, back_z, same_y, sem_zs.at[k], sem_zr.at[k], 1) for k in range(CHUNKS)]
+    image_y = [Pairs(c, sibling, turn_y, back_y, same_z, sem_ys.at[k], sem_yr.at[k]) for k in range(CHUNKS)]
+
+    def summed_over_planes(k):
+        total = part[lax.div(m * 5, 2) + k]
+        for d in range(1, NX):
+            arrival(parts.at[back_m[d], k], sem_ps.at[k, d], sem_pr.at[k, d], (r, back_m[d]))
+            total = total + parts[back_m[d], k]
+        picked_i[k] = mm(choose, total.astype(bf16)).astype(bf16).reshape(NZ, 32, 128)
+        hop_i[k, z] = picked_i[k, z]
+        image_z[k].send(lambda p, h: picked_i.at[k, p], hop_i.at[k, z], z)
+
+    def along_y(k):
+        image_z[k].wait(lambda p, h: hop_i.at[k, p], z)
+        turned_i[k] = mm(turn, hop_i[k].reshape(ROWS, 128)).astype(bf16).reshape(GROUP, 16, 128)
+        image[m, k, yc] = turned_i[k, yc]
+        image_y[k].send(lambda p, h: turned_i.at[k, p * NC + h], image.at[m, k, yc], y)
+
+    def over_planes(k):
+        image_y[k].wait(lambda p, h: image.at[m, k, p * NC + h], y)
+        for d in range(1, NX):
+            own = image.at[m, k]
+            sent.append(send(own, own, sem_qs.at[k, d], sem_qr.at[k, d], planes[d]))
+
     owner_col = to_col(owner_row)
     same = (owner_col == owner_row.astype(f32)) & (iota((128, 128), 1) < iota((128, 128), 0))
     rank = jnp.sum(jnp.where(same, 1.0, 0.0), -1, keepdims=True).astype(jnp.int32)
     owner = owner_col.astype(jnp.int32)
     spot = (owner >> 4) * 32 + rank * 16 + (owner & 15)
     fetch = hot(spot == iota((128, ROWS), 1))
+    held_y.wait(lambda p, h: hop_h.at[p * NC + h], y)
+    back = mm(swap_order(False), hop_h[...].reshape(ROWS, WINDOW)).astype(bf16)
+    turned_h[...] = back.reshape(NZ, 32, WINDOW)
+    hop_back[z] = turned_h[z]
+    held_z = Pairs(c, sibling, turn_z, back_z, same_y, sem_gs, sem_gr, 1)
+    held_z.send(lambda p, h: turned_h.at[p], hop_back.at[z], z)
+    ring_b.step(0)
+    summed_over_planes(0)
+    summed_over_planes(1)
+    ring_b.step(1)
+    along_y(0)
+    summed_over_planes(2)
+    held_z.wait(lambda p, h: hop_back.at[p], z)
+    held_in[m] = mm(fetch, hop_back[...].reshape(ROWS, WINDOW)).astype(bf16)
+    for d in range(1, NX):
+        sent.append(send(held_in.at[m], held_in.at[m], sem_xs.at[1, d], sem_xr.at[1, d], planes[d]))
+    ring_b.step(2)
+    along_y(1)
+    ring_b.step(3)
+    over_planes(0)
+    along_y(2)
+    tables[0].send(lambda p, h: idx_own.at[0], table.at[0, yc], y)
+    over_planes(1)
+    ring_b.finish(there)
+    for b in range(5):
+        span = slice(b * 256, (b + 1) * 256)
+        ordered[span, :] = mm(order[span, :], full_b[0].reshape(WIDTH, HALF)).astype(bf16)
+    over_planes(2)
+
+    gain = attn_gain[...].reshape(1, WIDTH)
     for d in range(1, NX):
         arrival(held_in.at[back_m[d]], sem_xs.at[1, d], sem_xr.at[1, d], (r, back_m[d]))
     for b in range(NX):
         o, w = OFFSETS[b], WIDTHS[b]
-        rows[0:128, o : o + w] = mm(fetch, held_in[b].reshape(ROWS, WINDOW)[:, 0:w])
+        rows[0:128, o : o + w] = held_in[b][:, 0:w].astype(f32)
     eye = hot(iota((LOCAL, LOCAL), 0) == iota((LOCAL, LOCAL), 1))
 
     def keys_and_values(count):
-        xk = mm(turned_cols[0:count, :], full_b[0].reshape(WIDTH, HALF)[:, 256:640])
+        xk = mm(normed[0:count, :], ordered[:, 256:640])
         xv = mm(normed[0:count, :], full_b[1].reshape(WIDTH, HALF)[:, 256:640])
         return (
             mm_t(eye, xk.astype(bf16)[:, 64:384]).astype(bf16),
             mm_t(eye, xv.astype(bf16)[:, 64:384]).astype(bf16),
         )
 
-    xn = norm(rows[0:128, :], gain)
-    normed[0:128, :] = xn
-    turned_cols[0:128, :] = mm(xn, order[...]).astype(bf16)
+    normed[0:128, :] = norm(rows[0:128, :], gain)
     fresh = keys_and_values(128)
     loads["keys"].wait()
     loads["values"].wait()
@@ -494,7 +515,8 @@
         for cached, new in ((keys, fresh[0]), (values, fresh[1])):
             cached[:, span] = jnp.where(hit, mm(new, put), cached[:, span].astype(f32)).astype(bf16)
 
-    named = hot(table[:, 0].reshape(128, 128) == r)
+    tables[0].wait(lambda p, h: table.at[0, p * NC + h], y)
+    named = hot(table[0].reshape(128, 128) == r)
     counts = mm_t(jnp.ones((8, 128), bf16), named)
     s0, s1 = iota((128, 128), 0), iota((128, 128), 1)
     ahead = hot((s0 & 7) * 16 + (s0 >> 3) < (s1 & 7) * 16 + (s1 >> 3))
@@ -516,16 +538,16 @@
     for b in range(NX):
         o, w = OFFSETS[b], WIDTHS[b]
         rows[:, o : o + w] = mm(take, text[:, o : o + w])
-    for d in range(1, NX):
-        arrival(image.at[back_m[d]], sem_xs.at[2, d], sem_xr.at[2, d], (r, back_m[d]))
-    for b in range(NX):
-        o, w = OFFSETS[b], WIDTHS[b]
-        rows[:, o : o + w] += mm(choose, image[b].reshape(ROWS, WINDOW)[:, 0:w])
-
-    xn = norm(rows[...], gain)
-    normed[...] = xn
-    turned_cols[...] = mm(xn, order[...]).astype(bf16)
-    queries = mm(turned_cols[...], full_b[0].reshape(WIDTH, HALF)[:, 0:384]).astype(bf16)
+    for k in range(CHUNKS):
+        for d in range(1, NX):
+            arrival(image.at[back_m[d], k], sem_qs.at[k, d], sem_qr.at[k, d], (r, back_m[d]))
+        for b in range(NX):
+            if k * 128 < WIDTHS[b]:
+                lanes = slice((FIRST[b] + k) * 128, (FIRST[b] + k + 1) * 128)
+                rows[:, lanes] += mm(choose, image[b, k].reshape(ROWS, 128))
+
+    normed[...] = norm(rows[...], gain)
+    queries = mm(normed[...], ordered[:, 0:384]).astype(bf16)
     new_keys, new_values = keys_and_values(ROWS)
     keys[:, WIDTH:] = new_keys
     values[:, WIDTH:] = new_values
@@ -549,23 +571,21 @@
             inverse = 1.0 / (jnp.sum(old, -1, keepdims=True) + jnp.sum(new, -1, keepdims=True))
             old, new = (old * inverse).astype(bf16), (new * inverse).astype(bf16)
             summed = mm_t(values[lanes, 0:WIDTH], old) + mm_t(values[lanes, WIDTH : WIDTH + count], new)
-            mixed_all[m, i, lanes, :] = jnp.where(live, summed, 0.0).astype(bf16)
+            mixed[i, lanes, :] = jnp.where(live, summed, 0.0).astype(bf16)
+        terms = mm(full_b[1].reshape(WIDTH, HALF)[:, 0:LOCAL], mixed[i])
+        product[i] = terms.reshape(NX, LOCAL, 128)
+        shares[i] = terms.astype(bf16).reshape(NX, LOCAL, 128)
         for d in range(1, NX):
-            half = mixed_all.at[m, i]
-            sent.append(send(half, half, sem_xs.at[4 + i, d], sem_xr.at[4 + i, d], planes[d]))
-
-    def product(plane, i):
-        return mm(out_cols[plane].reshape(LOCAL, WINDOW)[:, 0:LOCAL], mixed_all[plane, i])
-
-    for d in range(1, NX):
-        arrival(out_cols.at[back_m[d]], sem_xs.at[3, d], sem_xr.at[3, d], (r, back_m[d]))
+            src, dst = shares.at[i, planes[d][1]], others.at[i, m]
+            sent.append(send(src, dst, sem_xs.at[4 + i, d], sem_xr.at[4 + i, d], planes[d]))
+
     for i in range(2):
-        terms = product(m, i)
+        total = product[i, m]
         for d in range(1, NX):
-            arrival(mixed_all.at[back_m[d], i], sem_xs.at[4 + i, d], sem_xr.at[4 + i, d], (r, back_m[d]))
-            terms = terms + product(back_m[d], i)
-        result[:, i * 128 : (i + 1) * 128] = terms.astype(bf16)
-    for group_sent in (tables, held_y, held_z, image_z, image_y, ring_a, ring_b):
+            arrival(others.at[i, back_m[d]], sem_xs.at[4 + i, d], sem_xr.at[4 + i, d], (r, back_m[d]))
+            total = total + others[i, back_m[d]].astype(f32)
+        result[:, i * 128 : (i + 1) * 128] = total.astype(bf16)
+    for group_sent in (*tables, held_y, held_z, *image_z, *image_y, ring_a, ring_b):
         sent += group_sent.sent
     for copy in sent:
         copy.wait_send()
@@ -597,13 +617,11 @@
     recompute_pos,
 ):
     wb = jnp.concatenate([qkv_weight[0], qkv_weight[1], out_weight.T, qkv_weight[2]], 1)
-    k, p = np.arange(BLOCK)[:, None], np.arange(GROUP * PIECE)[None, :]
-    dense = jnp.asarray((p == k // SHARD * PIECE + k % SHARD).astype(np.float32)).astype(bf16)
     V = pltpu.VMEM
     result = pl.pallas_call(
         kernel,
         out_shape=SD((LOCAL, ROWS), bf16),
-        in_specs=[SM(), SM(), VM(), VM()] + [HB()] * 12,
+        in_specs=[SM(), SM(), VM(), VM()] + [HB()] * 11,
         out_specs=VM(),
         scratch_shapes=[
             V((SHARD, WIDTH), bf16),
@@ -623,42 +641,50 @@
             V((8, 128), jnp.int32),
             V((64, 128), jnp.int32),
             V((2, NZ, 128), jnp.int32),
-            V((GROUP, 2, NZ, 128), jnp.int32),
+            V((2, GROUP, NZ, 128), jnp.int32),
             V((WIDTH, WIDTH), bf16),
+            V((WIDTH, HALF), bf16),
             V((ROWS, WIDTH), bf16),
-            V((ROWS, WIDTH), bf16),
-            V((NX, 128, WINDOW), f32),
-            V((NX, 128, WINDOW), f32),
-            V((NZ, 32, WINDOW), bf16),
-            V((NZ, 32, WINDOW), bf16),
-            V((GROUP, 16, WINDOW), bf16),
-            V((NX, GROUP, 16, WINDOW), bf16),
+            V((128, WIDTH), bf16),
+            V((10, 128, 128), f32),
+            V((NX, CHUNKS, 128, 128), f32),
+            V((CHUNKS, NZ, 32, 128), bf16),
+            V((CHUNKS, NZ, 32, 128), bf16),
+            V((CHUNKS, GROUP, 16, 128), bf16),
+            V((NX, CHUNKS, GROUP, 16, 128), bf16),
             V((GROUP, 16, WINDOW), bf16),
             V((GROUP, 16, WINDOW), bf16),
             V((NZ, 32, WINDOW), bf16),
-            V((NX, NZ, 32, WINDOW), bf16),
-            V((NX, 2, BLOCK, WINDOW), bf16),
+            V((NZ, 32, WINDOW), bf16),
+            V((NX, 128, WINDOW), bf16),
             V((ROWS, WIDTH), f32),
-            V((NX, 2, LOCAL, 128), bf16),
-            DMA((12,)),
+            V((2, LOCAL, 128), bf16),
+            V((2, NX, LOCAL, 128), f32),
+            V((2, NX, LOCAL, 128), bf16),
+            V((2, NX, LOCAL, 128), bf16),
+            DMA((11,)),
             DMA((8, 2)),
             DMA((8, 2)),
             DMA((8, 2)),
             DMA((8, 2)),
             DMA((8,)),
             DMA((8,)),
+            DMA((2, 8, 2)),
+            DMA((2, 8, 2)),
             DMA((8, 2)),
             DMA((8, 2)),
             DMA((8, 2)),
             DMA((8, 2)),
-            DMA((8, 2)),
-            DMA((8, 2)),
-            DMA((8, 2)),
-            DMA((8, 2)),
-            DMA((8, 2)),
-            DMA((8, 2)),
-            DMA((6, NX)),
-            DMA((6, NX)),
+            DMA((CHUNKS, 8, 2)),
+            DMA((CHUNKS, 8, 2)),
+            DMA((CHUNKS, 8, 2)),
+            DMA((CHUNKS, 8, 2)),
+            DMA((CHUNKS, NX)),
+            DMA((CHUNKS, NX)),
+            DMA((CHUNKS, NX)),
+            DMA((CHUNKS, NX)),
+            DMA((8, NX)),
+            DMA((8, NX)),
             DMA((48,)),
             DMA((48,)),
             DMA((48,)),
@@ -678,7 +704,6 @@
         held_owner.reshape(1, 128),
         held_row,
         recompute_pos,
-        dense,
         patches[:, 0],
         held,
         text[0],

time: 109 us -> 98.4 us (0.903)
  Pallas kernels: 104 us -> 92.8 us
    pallas_call x1, Pallas kernels: 104 us -> 92.8 us  [local(): pl.pallas_call(kernel, out_shape=SD((LOCAL, ROWS), bf16), in_specs=[SM(),...]
where the time goes in v3:
time: 98.4 us; the launch traced here: 98.1 us
  Pallas kernels  92.8 us (94%)
  local copies, waits for them, and re-layouts  3.92 us (4%)
  between operations  1.33 us (1%)
    pallas_call x1, Pallas kernels, local(): pl.pallas_call(kernel, out_shape=SD((LOCAL, ROWS), bf16), in_specs=[SM(),...  92.8 us
    unnamed x4, local copies, waits for them, and re-layouts  2.29 us

profile of v3, /device:TPU:1, one launch (start us, length us, event | category | flops | bytes accessed | tf_op | source)
XLA Modules:
  0.0 98.1 jit_solution(1638306063748626512)
XLA Ops:
  1.3 0.9 fusion
  2.2 0.0 copy-start
  2.3 0.7 copy-done
  2.9 0.7 concatenate.3.wb_hbm
  3.6 92.8 %shard_map.154 = bf16[320,256]{1,0:T(8,128)(2,1)} custom-call(s32[1]{0:T(128)S(6)} %copy.28.image_pos, s32[1]{0:T(128)S(6)} %copy.29.text_len, f32[1280]{0:T(1024)} %vis_gain.1, f32[1280]{0:T(1024)} %attn_gain.1, bf16[10,1280]{1,0:T(8,128)(2,1)} %bitcast.28, bf16[10,1280]{1,0:T(8,128)(2,1)} %concatenate.3.wb_hbm, s32[1,128]{1,0:T(1,128)} %bitcast.30, ...), custom_call_target="tpu_custom_call" | custom-call | tf_op jit(solution)/shard_map/pallas_call | solution.py:621
  96.5 1.6 %copy.30 = bf16[1,256,320]{1,2,0:T(8,128)(2,1)} copy(bf16[1,256,320]{1,2,0:T(8,128)(2,1)} %bitcast.24) | data formatting | bytes 327680
  (2 shorter events, 0.0 us)
Async XLA Ops:
  2.2 0.7 copy-start

commit v4 on v3

--- a/solution.py
+++ b/solution.py
@@ -63,11 +63,15 @@
     ).wait_recv()
 
 
-def meet(devices):
-    barrier = pltpu.get_barrier_semaphore()
-    for device in devices:
-        pl.semaphore_signal(barrier, inc=1, device_id=device, device_id_type=MESH)
-    pl.semaphore_wait(barrier, len(devices))
+def departure(src, send_sem, recv_sem, device):
+    pltpu.make_async_remote_copy(
+        src_ref=src,
+        dst_ref=src,
+        send_sem=send_sem,
+        recv_sem=recv_sem,
+        device_id=device,
+        device_id_type=MESH,
+    ).wait_send()
 
 
 def iota(shape, dim):
@@ -106,8 +110,7 @@
     def __init__(self, full, own, c, place, near, sibling, sems):
         self.full, self.own, self.c, self.place = full, own, c, place
         self.near, self.sibling = near, sibling
-        self.ssem, self.rsem = sems
-        self.sent = []
+        self.chunk_ssem, self.chunk_rsem, self.block_ssem, self.block_rsem = sems
 
     def block(self, half, number):
         return self.full.at[half, lax.rem(number + 2 * NZ, NZ)]
@@ -115,8 +118,11 @@
     def chunk(self, ref, k):
         return ref.at[pl.ds(k * self.ROWS, self.ROWS)]
 
-    def push(self, src, dst, slot, device):
-        self.sent.append(send(src, dst, self.ssem.at[slot], self.rsem.at[slot], device))
+    def push(self, part, slot, device):
+        send(part, part, self.chunk_ssem, self.chunk_rsem.at[slot], device)
+
+    def hand(self, block):
+        send(block, block, self.block_ssem, self.block_rsem, self.sibling)
 
     def start(self, value):
         self.full[self.c, self.place] = value
@@ -124,8 +130,8 @@
         for k in range(self.CHUNKS):
             for side in range(2):
                 part = self.chunk(own, k)
-                self.push(part, part, side * 20 + k, self.near[side])
-        self.push(own, own, 40, self.sibling)
+                self.push(part, side * 20 + k, self.near[side])
+        self.hand(own)
 
     def step(self, s):
         sides = (-1, 1)
@@ -135,18 +141,19 @@
                     continue
                 slot = side * 20 + s * 5 + k
                 part = self.chunk(self.block(self.c, self.place + sides[side] * (1 + s)), k)
-                arrival(part, self.ssem.at[slot], self.rsem.at[slot], self.near[side])
+                arrival(part, self.chunk_ssem, self.chunk_rsem.at[slot], self.near[side])
                 if s < 2 or (s == 2 and (k < 3) == (side == 0)):
-                    self.push(part, part, slot + 5, self.near[side])
+                    self.push(part, slot + 5, self.near[side])
         for side in range(2):
             if s < 3 or side == 0:
-                got = self.block(self.c, self.place + sides[side] * (1 + s))
-                self.push(got, got, 41 + 2 * s + side, self.sibling)
-
-    def finish(self, place):
-        for slot, shift in ((40, 0), (41, -1), (42, 1), (43, -2), (44, 2), (45, -3), (46, 3), (47, -4)):
-            got = self.block(1 - self.c, place + shift)
-            arrival(got, self.ssem.at[slot], self.rsem.at[slot], self.sibling)
+                self.hand(self.block(self.c, self.place + sides[side] * (1 + s)))
+
+    def finish(self):
+        arrival(self.full.at[1 - self.c], self.block_ssem, self.block_rsem, self.sibling)
+
+    def drain(self):
+        departure(self.full.at[0, pl.ds(0, 7)], self.chunk_ssem, self.block_rsem, self.sibling)
+        departure(self.full.at[0], self.block_ssem, self.block_rsem, self.sibling)
 
 
 def to_col(row):
@@ -158,7 +165,6 @@
     def __init__(self, c, sibling, turn, back, device, ssem, rsem, cores=NC):
         self.c, self.sibling, self.turn, self.back = c, sibling, turn, back
         self.device, self.ssem, self.rsem, self.cores = device, ssem, rsem, cores
-        self.sent = []
 
     def spans(self):
         for d in range(1, 8):
@@ -170,19 +176,15 @@
             if d not in distances:
                 continue
             to = self.turn[d]
-            self.sent.append(
-                send(pick(to, h), dst, self.ssem.at[d, k], self.rsem.at[d, k], self.device(to, h))
-            )
+            send(pick(to, h), dst, self.ssem, self.rsem, self.device(to, h))
         if self.cores == 2 and 0 in distances:
-            src = pick(own, 1 - self.c)
-            self.sent.append(send(src, dst, self.ssem.at[0, 0], self.rsem.at[0, 0], self.sibling))
-
-    def wait(self, spot, own):
-        for d, k, h in self.spans():
-            to = self.back[d]
-            arrival(spot(to, h), self.ssem.at[d, k], self.rsem.at[d, k], self.device(to, h))
-        if self.cores == 2:
-            arrival(spot(own, 1 - self.c), self.ssem.at[0, 0], self.rsem.at[0, 0], self.sibling)
+            send(pick(own, 1 - self.c), dst, self.ssem, self.rsem, self.sibling)
+
+    def wait(self, whole):
+        arrival(whole, self.ssem, self.rsem, self.sibling)
+
+    def drain(self, whole):
+        departure(whole, self.ssem, self.rsem, self.sibling)
 
 
 def kernel(
@@ -241,32 +243,10 @@
     shares,
     others,
     local,
-    sem_as,
-    sem_ar,
-    sem_bs,
-    sem_br,
-    sem_is,
-    sem_ir,
-    sem_ts,
-    sem_tr,
-    sem_hs,
-    sem_hr,
-    sem_gs,
-    sem_gr,
-    sem_zs,
-    sem_zr,
-    sem_ys,
-    sem_yr,
-    sem_ps,
-    sem_pr,
-    sem_qs,
-    sem_qr,
-    sem_xs,
-    sem_xr,
-    sem_ras,
-    sem_rar,
-    sem_rbs,
-    sem_rbr,
+    snd,
+    rcv,
+    chunk_a,
+    chunk_b,
 ):
     r, m, z, y, c = coords()
     yc = y * NC + c
@@ -319,38 +299,29 @@
     dest_row, owner_row = small[0], small[1]
     idx[...] = jnp.concatenate([dest_row, owner_row * 128 + small[2], jnp.zeros((6, 128), jnp.int32)], 0)
     pl.semaphore_wait(barrier, len(peers))
-    sent = []
 
     mine = pl.ds(pl.multiple_of(z * 8, 8), 8)
     idx_stage[mine, :] = idx[...]
     for d in range(1, NZ):
-        sent.append(send(idx, idx_stage.at[mine], sem_is.at[d], sem_ir.at[d], same_y(turn_z[d], c)))
+        send(idx, idx_stage.at[mine], snd.at[2], rcv.at[2], same_y(turn_z[d], c))
 
     group = (1 - c) * z + c * y
-    back_g = [lax.rem(group + 8 - d, 8) for d in range(8)]
-
-    def spread(n, stage, ssem, rsem):
+
+    def spread(n, stage):
         kept = jnp.where(c == 0, piece[n, 0].astype(f32), piece[n, 1].astype(f32))
         stage[group * NC + c] = kept.astype(bf16)
         there = (1 - c) * y + c * z
-        spot = stage.at[there * NC + c]
-        sent.append(send(piece.at[n, 1 - c], spot, ssem.at[0, 0], rsem.at[0, 0], sibling))
+        send(piece.at[n, 1 - c], stage.at[there * NC + c], snd.at[n], rcv.at[n], sibling)
         for d in range(1, 8):
-            spot = stage.at[z * NC + c]
-            sent.append(send(piece.at[n, 0], spot, ssem.at[d, 0], rsem.at[d, c], same_y(turn_z[d], 0)))
-            spot = stage.at[y * NC + c]
-            sent.append(send(piece.at[n, 1], spot, ssem.at[d, 1], rsem.at[d, c], same_z(turn_y[d], 1)))
-
-    def gathered(stage, ssem, rsem):
-        arrival(stage.at[group * NC + 1 - c], ssem.at[0, 0], rsem.at[0, 0], sibling)
-        for d in range(1, 8):
-            for k in range(NC):
-                spot = stage.at[back_g[d] * NC + k]
-                arrival(spot, ssem.at[d, 0], rsem.at[d, k], sibling)
+            send(piece.at[n, 0], stage.at[z * NC + c], snd.at[n], rcv.at[n], same_y(turn_z[d], 0))
+            send(piece.at[n, 1], stage.at[y * NC + c], snd.at[n], rcv.at[n], same_z(turn_y[d], 1))
+
+    def gathered(n, stage):
+        arrival(stage.at[pl.ds(0, GROUP - 1)], snd.at[n], rcv.at[n], sibling)
         return mm(dense[...], stage[...].reshape(GROUP * PIECE, HALF)).astype(bf16)
 
-    spread(0, stage_a, sem_as, sem_ar)
-    spread(1, stage_b, sem_bs, sem_br)
+    spread(0, stage_a)
+    spread(1, stage_b)
 
     loads["patch"].wait()
     xn = norm(patch[...].astype(f32), vis_gain[...].reshape(1, WIDTH))
@@ -364,29 +335,26 @@
     k = iota((BLOCK, 1), 0)
     dense[...] = hot(iota((BLOCK, GROUP * PIECE), 1) == lax.div(k, SHARD) * PIECE + lax.rem(k, SHARD))
 
-    for d in range(1, NZ):
-        got = idx_stage.at[pl.ds(pl.multiple_of(back_z[d] * 8, 8), 8)]
-        arrival(got, sem_is.at[d], sem_ir.at[d], same_y(back_z[d], c))
+    arrival(idx_stage.at[pl.ds(0, 56)], snd.at[2], rcv.at[2], sibling)
     for which in range(2):
         idx_own[which] = idx_stage[pl.ds(which, NZ, stride=8), :]
     place = (1 - c) * y + c * z
-    there = (1 - c) * z + c * y
 
     def ring_device(p):
         return ((1 - c) * (z * GROUP + p * NC) + c * (p * GROUP + y * NC + 1), m)
 
     near = [ring_device(lax.rem(place + 1, 8)), ring_device(lax.rem(place + 7, 8))]
-    ring_a = Ring(full_a, None, c, place, near, sibling, (sem_ras, sem_rar))
-    ring_b = Ring(full_b, None, c, place, near, sibling, (sem_rbs, sem_rbr))
+    ring_a = Ring(full_a, None, c, place, near, sibling, (snd.at[22], chunk_a, snd.at[24], rcv.at[22]))
+    ring_b = Ring(full_b, None, c, place, near, sibling, (snd.at[23], chunk_b, snd.at[25], rcv.at[23]))
     tables = []
     for n in range(2):
         table[n, yc] = idx_own[n]
-        tables.append(Pairs(c, sibling, turn_y, back_y, same_z, sem_ts.at[n], sem_tr.at[n]))
+        tables.append(Pairs(c, sibling, turn_y, back_y, same_z, snd.at[3 + n], rcv.at[3 + n]))
     tables[1].send(lambda p, h: idx_own.at[1], table.at[1, yc], y)
-    ring_a.start(gathered(stage_a, sem_as, sem_ar))
+    ring_a.start(gathered(0, stage_a))
     ring_a.step(0)
 
-    tables[1].wait(lambda p, h: table.at[1, p * NC + h], y)
+    tables[1].wait(table.at[1, pl.ds(0, 15)])
     code = table[1]
     asked = (code >> 7) == r
     row = (code & 127).astype(f32)
@@ -401,13 +369,13 @@
     loads["held"].wait()
     picked_h[...] = mm(pick, held[:, pl.ds(base, WINDOW)]).astype(bf16).reshape(GROUP, 16, WINDOW)
     hop_h[yc] = picked_h[yc]
-    held_y = Pairs(c, sibling, turn_y, back_y, same_z, sem_hs, sem_hr)
+    held_y = Pairs(c, sibling, turn_y, back_y, same_z, snd.at[5], rcv.at[5])
     for step, distances in ((1, (0, 1, 2)), (2, (3, 4, 5)), (3, (6, 7))):
         held_y.send(lambda p, h: picked_h.at[p * NC + h], hop_h.at[yc], y, distances)
         ring_a.step(step)
-    ring_b.start(gathered(stage_b, sem_bs, sem_br))
-
-    ring_a.finish(there)
+    ring_b.start(gathered(1, stage_b))
+
+    ring_a.finish()
     left = mm(turned_cols[...], full_a[0].reshape(WIDTH, HALF))
     for b in range(5):
         part[b] = left[:, b * 128 : (b + 1) * 128]
@@ -417,7 +385,7 @@
     for k in range(CHUNKS):
         for d in range(1, NX):
             src = part.at[lax.div(planes[d][1] * 5, 2) + k]
-            sent.append(send(src, parts.at[m, k], sem_ps.at[k, d], sem_pr.at[k, d], planes[d]))
+            send(src, parts.at[m, k], snd.at[13 + k], rcv.at[13 + k], planes[d])
 
     dest_col = to_col(dest_row)
     earlier = (dest_col == dest_row.astype(f32)) & (iota((128, 128), 0) < iota((128, 128), 1))
@@ -427,29 +395,29 @@
     slot = ((q >> 4) & 1).astype(f32)
     choose = hot((dest_row == target) & (rank == slot))
     turn = swap_order(True)
-    image_z = [Pairs(c, sibling, turn_z, back_z, same_y, sem_zs.at[k], sem_zr.at[k], 1) for k in range(CHUNKS)]
-    image_y = [Pairs(c, sibling, turn_y, back_y, same_z, sem_ys.at[k], sem_yr.at[k]) for k in range(CHUNKS)]
+    image_z = [Pairs(c, sibling, turn_z, back_z, same_y, snd.at[7 + k], rcv.at[7 + k], 1) for k in range(CHUNKS)]
+    image_y = [Pairs(c, sibling, turn_y, back_y, same_z, snd.at[10 + k], rcv.at[10 + k]) for k in range(CHUNKS)]
 
     def summed_over_planes(k):
+        arrival(parts.at[0], snd.at[13 + k], rcv.at[13 + k], sibling)
         total = part[lax.div(m * 5, 2) + k]
         for d in range(1, NX):
-            arrival(parts.at[back_m[d], k], sem_ps.at[k, d], sem_pr.at[k, d], (r, back_m[d]))
             total = total + parts[back_m[d], k]
         picked_i[k] = mm(choose, total.astype(bf16)).astype(bf16).reshape(NZ, 32, 128)
         hop_i[k, z] = picked_i[k, z]
         image_z[k].send(lambda p, h: picked_i.at[k, p], hop_i.at[k, z], z)
 
     def along_y(k):
-        image_z[k].wait(lambda p, h: hop_i.at[k, p], z)
+        image_z[k].wait(hop_i.at[k, pl.ds(0, 7)])
         turned_i[k] = mm(turn, hop_i[k].reshape(ROWS, 128)).astype(bf16).reshape(GROUP, 16, 128)
         image[m, k, yc] = turned_i[k, yc]
         image_y[k].send(lambda p, h: turned_i.at[k, p * NC + h], image.at[m, k, yc], y)
 
     def over_planes(k):
-        image_y[k].wait(lambda p, h: image.at[m, k, p * NC + h], y)
+        image_y[k].wait(image.at[m, k, pl.ds(0, 15)])
         for d in range(1, NX):
             own = image.at[m, k]
-            sent.append(send(own, own, sem_qs.at[k, d], sem_qr.at[k, d], planes[d]))
+            send(own, own, snd.at[16 + k], rcv.at[16 + k], planes[d])
 
     owner_col = to_col(owner_row)
     same = (owner_col == owner_row.astype(f32)) & (iota((128, 128), 1) < iota((128, 128), 0))
@@ -457,11 +425,11 @@
     owner = owner_col.astype(jnp.int32)
     spot = (owner >> 4) * 32 + rank * 16 + (owner & 15)
     fetch = hot(spot == iota((128, ROWS), 1))
-    held_y.wait(lambda p, h: hop_h.at[p * NC + h], y)
+    held_y.wait(hop_h.at[pl.ds(0, 15)])
     back = mm(swap_order(False), hop_h[...].reshape(ROWS, WINDOW)).astype(bf16)
     turned_h[...] = back.reshape(NZ, 32, WINDOW)
     hop_back[z] = turned_h[z]
-    held_z = Pairs(c, sibling, turn_z, back_z, same_y, sem_gs, sem_gr, 1)
+    held_z = Pairs(c, sibling, turn_z, back_z, same_y, snd.at[6], rcv.at[6], 1)
     held_z.send(lambda p, h: turned_h.at[p], hop_back.at[z], z)
     ring_b.step(0)
     summed_over_planes(0)
@@ -469,10 +437,10 @@
     ring_b.step(1)
     along_y(0)
     summed_over_planes(2)
-    held_z.wait(lambda p, h: hop_back.at[p], z)
+    held_z.wait(hop_back.at[pl.ds(0, 7)])
     held_in[m] = mm(fetch, hop_back[...].reshape(ROWS, WINDOW)).astype(bf16)
     for d in range(1, NX):
-        sent.append(send(held_in.at[m], held_in.at[m], sem_xs.at[1, d], sem_xr.at[1, d], planes[d]))
+        send(held_in.at[m], held_in.at[m], snd.at[19], rcv.at[19], planes[d])
     ring_b.step(2)
     along_y(1)
     ring_b.step(3)
@@ -480,15 +448,14 @@
     along_y(2)
     tables[0].send(lambda p, h: idx_own.at[0], table.at[0, yc], y)
     over_planes(1)
-    ring_b.finish(there)
+    ring_b.finish()
+    over_planes(2)
     for b in range(5):
         span = slice(b * 256, (b + 1) * 256)
         ordered[span, :] = mm(order[span, :], full_b[0].reshape(WIDTH, HALF)).astype(bf16)
-    over_planes(2)
 
     gain = attn_gain[...].reshape(1, WIDTH)
-    for d in range(1, NX):
-        arrival(held_in.at[back_m[d]], sem_xs.at[1, d], sem_xr.at[1, d], (r, back_m[d]))
+    arrival(held_in.at[pl.ds(0, 3)], snd.at[19], rcv.at[19], sibling)
     for b in range(NX):
         o, w = OFFSETS[b], WIDTHS[b]
         rows[0:128, o : o + w] = held_in[b][:, 0:w].astype(f32)
@@ -515,7 +482,7 @@
         for cached, new in ((keys, fresh[0]), (values, fresh[1])):
             cached[:, span] = jnp.where(hit, mm(new, put), cached[:, span].astype(f32)).astype(bf16)
 
-    tables[0].wait(lambda p, h: table.at[0, p * NC + h], y)
+    tables[0].wait(table.at[0, pl.ds(0, 15)])
     named = hot(table[0].reshape(128, 128) == r)
     counts = mm_t(jnp.ones((8, 128), bf16), named)
     s0, s1 = iota((128, 128), 0), iota((128, 128), 1)
@@ -539,8 +506,7 @@
         o, w = OFFSETS[b], WIDTHS[b]
         rows[:, o : o + w] = mm(take, text[:, o : o + w])
     for k in range(CHUNKS):
-        for d in range(1, NX):
-            arrival(image.at[back_m[d], k], sem_qs.at[k, d], sem_qr.at[k, d], (r, back_m[d]))
+        arrival(image.at[0], snd.at[16 + k], rcv.at[16 + k], sibling)
         for b in range(NX):
             if k * 128 < WIDTHS[b]:
                 lanes = slice((FIRST[b] + k) * 128, (FIRST[b] + k + 1) * 128)
@@ -577,18 +543,29 @@
         shares[i] = terms.astype(bf16).reshape(NX, LOCAL, 128)
         for d in range(1, NX):
             src, dst = shares.at[i, planes[d][1]], others.at[i, m]
-            sent.append(send(src, dst, sem_xs.at[4 + i, d], sem_xr.at[4 + i, d], planes[d]))
+            send(src, dst, snd.at[20 + i], rcv.at[20 + i], planes[d])
 
     for i in range(2):
+        arrival(others.at[i, pl.ds(0, 3)], snd.at[20 + i], rcv.at[20 + i], sibling)
         total = product[i, m]
         for d in range(1, NX):
-            arrival(others.at[i, back_m[d]], sem_xs.at[4 + i, d], sem_xr.at[4 + i, d], (r, back_m[d]))
             total = total + others[i, back_m[d]].astype(f32)
         result[:, i * 128 : (i + 1) * 128] = total.astype(bf16)
-    for group_sent in (*tables, held_y, held_z, *image_z, *image_y, ring_a, ring_b):
-        sent += group_sent.sent
-    for copy in sent:
-        copy.wait_send()
+    departure(idx_stage.at[pl.ds(0, 56)], snd.at[2], rcv.at[2], sibling)
+    departure(held_in.at[pl.ds(0, 3)], snd.at[19], rcv.at[19], sibling)
+    for n, stage in ((0, stage_a), (1, stage_b)):
+        departure(stage.at[pl.ds(0, GROUP - 1)], snd.at[n], rcv.at[n], sibling)
+        tables[n].drain(table.at[n, pl.ds(0, 15)])
+        departure(others.at[n, pl.ds(0, 3)], snd.at[20 + n], rcv.at[20 + n], sibling)
+    held_y.drain(hop_h.at[pl.ds(0, 15)])
+    held_z.drain(hop_back.at[pl.ds(0, 7)])
+    for k in range(CHUNKS):
+        departure(parts.at[0], snd.at[13 + k], rcv.at[13 + k], sibling)
+        image_z[k].drain(hop_i.at[k, pl.ds(0, 7)])
+        image_y[k].drain(turned_i.at[k, pl.ds(0, 15)])
+        departure(image.at[0], snd.at[16 + k], rcv.at[16 + k], sibling)
+    ring_a.drain()
+    ring_b.drain()
 
 
 VM = functools.partial(pl.BlockSpec, memory_space=pltpu.VMEM)
@@ -663,32 +640,10 @@
             V((2, NX, LOCAL, 128), bf16),
             V((2, NX, LOCAL, 128), bf16),
             DMA((11,)),
-            DMA((8, 2)),
-            DMA((8, 2)),
-            DMA((8, 2)),
-            DMA((8, 2)),
-            DMA((8,)),
-            DMA((8,)),
-            DMA((2, 8, 2)),
-            DMA((2, 8, 2)),
-            DMA((8, 2)),
-            DMA((8, 2)),
-            DMA((8, 2)),
-            DMA((8, 2)),
-            DMA((CHUNKS, 8, 2)),
-            DMA((CHUNKS, 8, 2)),
-            DMA((CHUNKS, 8, 2)),
-            DMA((CHUNKS, 8, 2)),
-            DMA((CHUNKS, NX)),
-            DMA((CHUNKS, NX)),
-            DMA((CHUNKS, NX)),
-            DMA((CHUNKS, NX)),
-            DMA((8, NX)),
-            DMA((8, NX)),
-            DMA((48,)),
-            DMA((48,)),
-            DMA((48,)),
-            DMA((48,)),
+            DMA((26,)),
+            DMA((24,)),
+            DMA((40,)),
+            DMA((40,)),
         ],
         compiler_params=pltpu.CompilerParams(
             collective_id=1, has_side_effects=True, vmem_limit_bytes=56 * 1024 * 1024

time: 98.4 us -> 93.1 us (0.946)
  Pallas kernels: 92.8 us -> 87.5 us
    pallas_call x1, Pallas kernels: 92.8 us -> 87.5 us  [local(): pl.pallas_call(kernel, out_shape=SD((LOCAL, ROWS), bf16), in_specs=[SM(),...]
where the time goes in v4:
time: 93.1 us; the launch traced here: 92.7 us
  Pallas kernels  87.5 us (94%)
  local copies, waits for them, and re-layouts  3.92 us (4%)
  between operations  1.33 us (1%)
    pallas_call x1, Pallas kernels, local(): pl.pallas_call(kernel, out_shape=SD((LOCAL, ROWS), bf16), in_specs=[SM(),...  87.5 us
    unnamed x4, local copies, waits for them, and re-layouts  2.29 us

profile of v4, /device:TPU:1, one launch (start us, length us, event | category | flops | bytes accessed | tf_op | source)
XLA Modules:
  0.0 92.7 jit_solution(8331476805480048671)
XLA Ops:
  1.3 0.9 fusion
  2.2 0.0 copy-start
  2.3 0.7 copy-done
  2.9 0.7 concatenate.3.wb_hbm
  3.6 87.5 %shard_map.154 = bf16[320,256]{1,0:T(8,128)(2,1)} custom-call(s32[1]{0:T(128)S(6)} %copy.28.image_pos, s32[1]{0:T(128)S(6)} %copy.29.text_len, f32[1280]{0:T(1024)} %vis_gain.1, f32[1280]{0:T(1024)} %attn_gain.1, bf16[10,1280]{1,0:T(8,128)(2,1)} %bitcast.28, bf16[10,1280]{1,0:T(8,128)(2,1)} %concatenate.3.wb_hbm, s32[1,128]{1,0:T(1,128)} %bitcast.30, ...), custom_call_target="tpu_custom_call" | custom-call | tf_op jit(solution)/shard_map/pallas_call | solution.py:598
  91.1 1.6 %copy.30 = bf16[1,256,320]{1,2,0:T(8,128)(2,1)} copy(bf16[1,256,320]{1,2,0:T(8,128)(2,1)} %bitcast.24) | data formatting | bytes 327680
  (2 shorter events, 0.0 us)
Async XLA Ops:
  2.2 0.7 copy-start
